TPU v7x, 32 devices: a whole 2x2x4 slice. The times are simulated.
32 devices in a mesh: pair: 4 (over y, x), virt: 8 (over z, core).
Axes of the slice: x: 2, y: 2, z: 4, core: 2. Of those that a mesh axis runs over, the one named last changes fastest.
Arguments:
- amplitudes: float32 [480, 12288], P('pair', 'virt'), may hold values from -6 to 6
- integrals: float32 [8192, 12288], P('pair', 'virt'), may hold values from -0.0546875 to 0.0546875
- eps_occ: float32 [120], replicated, may hold values from -2.5 to -0.3
- eps_vir: float32 [128], replicated, may hold values from 0.3 to 3
- pair_list: int32 [480, 2], P('pair'), may hold values from 0 to 119, as said below
Outputs:
- ladder: float32 [480, 8192], P('pair', 'virt')
- update: float32 [480, 8192], P('pair', 'virt')
Inputs may be any that keep to these rules, and one draw needn't show every extreme that they name: `pair_list`: each row (i, j) has i < j; pairs may repeat.
All inputs are finite; a program needn't handle non-finite values.
Results may differ from a plain program's by a relative error of at most 0.000071.
Values sent between devices are 32-bit elements; how exact they have to be, the bound alone decides.
A program may use at most 64 MiB of HBM per device.

v0:
```python
import functools

import jax
import jax.numpy as jnp
from jax import lax
from jax.experimental import pallas as pl
from jax.experimental.pallas import tpu as pltpu
from jax.sharding import PartitionSpec as P

MESH = pl.DeviceIdType.MESH
LANES = 128


def antisymmetrize(partial_value, tile_width):
    blocks = partial_value.reshape(partial_value.shape[0], 2, tile_width, tile_width)
    mirrored = jnp.swapaxes(blocks[:, ::-1], 2, 3)
    return (blocks - mirrored).reshape(partial_value.shape)


def pair_energies(eps_occ, pair_list):
    occ_ids = lax.broadcasted_iota(jnp.int32, (1, 1, eps_occ.shape[0]), 2)
    one_hot = pair_list[:, :, None] == occ_ids
    return jnp.sum(jnp.where(one_hot, eps_occ[None, None, :], jnp.float32(0.0)), axis=(1, 2))


def sum_to_owners(antisym):
    return lax.psum_scatter(antisym, "virt", scatter_dimension=1, tiled=True)


def updated(ladder, eps_occ, eps_vir, pair_list):
    tile_width = eps_vir.shape[0] // 2
    column_count = ladder.shape[1]
    energy_tiles = eps_vir.reshape(2, tile_width)
    virt_energy = (energy_tiles[:, :, None] + energy_tiles[::-1][:, None, :]).reshape(
        2 * tile_width * tile_width
    )
    local_energy = lax.dynamic_slice_in_dim(
        virt_energy, lax.axis_index("virt") * column_count, column_count
    )
    pair_energy = pair_energies(eps_occ, pair_list)
    return ladder / (pair_energy[:, None] - local_energy[None, :])


def any_mesh_body(amplitudes, integrals, eps_occ, eps_vir, pair_list):
    tile_width = eps_vir.shape[0] // 2
    by_pairs = lax.dot_general(
        lax.all_gather(amplitudes, "pair", axis=0, tiled=True),
        integrals,
        (((1,), (1,)), ((), ())),
        precision=lax.Precision.HIGHEST,
        preferred_element_type=jnp.float32,
    )
    partial_value = lax.all_to_all(by_pairs, "pair", split_axis=0, concat_axis=1, tiled=True)
    ladder = sum_to_owners(antisymmetrize(partial_value, tile_width))
    return (ladder, updated(ladder, eps_occ, eps_vir, pair_list))


def split(value):
    high = value.astype(jnp.bfloat16)
    return high, (value - high.astype(jnp.float32)).astype(jnp.bfloat16)


def times(left, right):
    return lax.dot_general(
        left, right, (((1,), (1,)), ((), ())), preferred_element_type=jnp.float32
    )


def ladder_kernel(
    h, amp_ref, int_ref, out_ref, stage, int_high, int_low, blocks, weights, ct_ref,
    got, summed, rows, diff, below, above, upward, downward, kept, other, placed,
    stage_sem, amp_send, amp_recv,
    core_send, core_recv, pair_send, pair_recv, up_send, up_recv, down_send, down_recv,
    last_send, last_recv,
):
    r = lax.axis_index("pair")
    v = lax.axis_index("virt")
    z = v // 2
    c = v % 2
    mate = v + 1 - 2 * c
    x = r % 2
    y = r // 2
    peers = (y * 2 + (1 - x), (1 - y) * 2 + x, (1 - y) * 2 + (1 - x))
    count, depth = amp_ref.shape
    cut = count // 16 * 8
    parts = (pl.ds(0, cut), pl.ds(cut, count - cut))
    step = stage.shape[1]
    steps = int_ref.shape[0] // step

    def stage_copy(t):
        return pltpu.make_async_copy(
            int_ref.at[pl.ds(pl.multiple_of(t * step, 8), step)],
            stage.at[t % 2],
            stage_sem.at[t % 2],
        )

    stage_copy(0).start()
    stage_copy(1).start()

    barrier = pltpu.get_barrier_semaphore()
    pl.semaphore_signal(barrier, inc=1, device_id={"virt": mate}, device_id_type=MESH)
    for peer in peers:
        pl.semaphore_signal(barrier, inc=1, device_id={"pair": peer}, device_id_type=MESH)

    @pl.when(z < 3)
    def _():
        pl.semaphore_signal(barrier, inc=1, device_id={"virt": v + 2}, device_id_type=MESH)

    @pl.when(z > 0)
    def _():
        pl.semaphore_signal(barrier, inc=1, device_id={"virt": v - 2}, device_id_type=MESH)

    inner = jnp.logical_and(z > 0, z < 3)

    @pl.when(inner)
    def _():
        pl.semaphore_wait(barrier, 6)

    @pl.when(jnp.logical_not(inner))
    def _():
        pl.semaphore_wait(barrier, 5)

    def amp_copy(d, part):
        return pltpu.make_async_remote_copy(
            src_ref=amp_ref.at[parts[part]],
            dst_ref=blocks.at[d, parts[part]],
            send_sem=amp_send.at[d, part],
            recv_sem=amp_recv.at[d, part],
            device_id={"pair": peers[d]},
            device_id_type=MESH,
        )

    def pass_on(d):
        return pltpu.make_async_remote_copy(
            src_ref=blocks.at[d, parts[d]],
            dst_ref=blocks.at[2, parts[d]],
            send_sem=amp_send.at[2, d],
            recv_sem=amp_recv.at[2, d],
            device_id={"pair": peers[1 - d]},
            device_id_type=MESH,
        )

    for late in range(2):
        for d in range(2):
            amp_copy(d, d if late == 0 else 1 - d).start()

    def weigh(source, high_at, low_at):
        wide = 2 * LANES

        @pl.loop(0, depth // wide)
        def _(k):
            columns = pl.ds(pl.multiple_of(k * wide, wide), wide)
            value = source[:, columns]
            if count < LANES:
                value = jnp.concatenate(
                    [value, jnp.zeros((LANES - count, wide), jnp.float32)], axis=0
                )
            high, low = split(value)
            weights[pl.ds(high_at * LANES, LANES), columns] = high
            weights[pl.ds(low_at * LANES, LANES), columns] = low

    def keep(t, size, lanes, value):
        per = size // (4 * h)
        i = t // (h // per)
        at = pl.multiple_of(t % (h // per) * per, per)
        ct_ref[i, pl.ds(at, per), :, :, :, lanes] = value.reshape(per, 2, 2, h, value.shape[1])

    def one_block(high, low, at):
        both = times(high, weights[pl.ds(at * LANES, 2 * LANES), :])
        rest = times(low, weights[pl.ds(at * LANES, LANES), :])
        return both[:, :LANES] + both[:, LANES:] + rest

    weigh(amp_ref, 0, 1)

    @pl.loop(0, steps)
    def _(t):
        stage_copy(t).wait()
        high, low = split(stage[t % 2])
        at = pl.ds(pl.multiple_of(t * step, 16), step)
        int_high[at, :] = high
        int_low[at, :] = low

        @pl.when(t + 2 < steps)
        def _():
            stage_copy(t + 2).start()

        keep(t, step, pl.ds(3 * LANES, LANES), one_block(int_high[at, :], int_low[at, :], 0))

    for d in range(2):
        amp_copy(d, d).wait_recv()
        pass_on(d).start()

    order = (peers[2], peers[0], peers[1], r)

    def core_copy(n, i):
        return pltpu.make_async_remote_copy(
            src_ref=ct_ref.at[i, :, :, (1 - c + i) % 2, :, pl.ds(n * LANES, LANES)],
            dst_ref=got.at[n, i],
            send_sem=core_send.at[n, i],
            recv_sem=core_recv.at[n, i],
            device_id={"virt": mate},
            device_id_type=MESH,
        )

    def pair_copy(n, piece):
        bh = jnp.where(piece == 0, 1 - x, x) if n == 1 else piece
        return pltpu.make_async_remote_copy(
            src_ref=summed.at[n, :, bh],
            dst_ref=rows.at[r, :, bh],
            send_sem=pair_send.at[n, piece],
            recv_sem=pair_recv.at[n, piece],
            device_id={"pair": order[n]},
            device_id_type=MESH,
        )

    def pair_arrived(n, piece):
        pair_copy(n, piece).wait_recv()

    def core_start(n):
        for i in range(2):
            core_copy(n, i).start()

    half = steps // 4

    def core_add(n):
        lanes = pl.ds(n * LANES, LANES)
        for i in range(2):
            core_copy(n, i).wait_recv()

            @pl.loop(0, h, unroll=4)
            def _(a):
                for bh in range(2):
                    total = ct_ref[i, a, bh, (c + i) % 2, :, lanes] + got[n, i, a, bh]
                    if n < 3:
                        summed[n, i * h + a, bh] = total
                    else:
                        rows[r, i * h + a, bh] = total

    core_start(3)
    for d in range(2):
        amp_copy(d, 1 - d).wait_recv()
        weigh(blocks.at[d], 4 + d, 6 + d)
    big = 2 * step

    for i in range(2):

        @pl.loop(i * half, (i + 1) * half)
        def _(t):
            at = pl.ds(pl.multiple_of(t * big, 16), big)
            near_high = weights[pl.ds(4 * LANES, 2 * LANES), :]
            near_low = weights[pl.ds(6 * LANES, 2 * LANES), :]
            value = times(int_high[at, :], near_high) + times(int_high[at, :], near_low)
            value = value + times(int_low[at, :], near_high)
            keep(t, big, pl.ds(LANES, 2 * LANES), value)

        core_copy(1, i).start()
        core_copy(2, i).start()

    core_add(1)
    pair_copy(1, 0).start()
    core_add(2)
    pair_copy(2, 0).start()
    pair_copy(2, 1).start()
    pair_copy(1, 1).start()
    core_add(3)
    for d in range(2):
        pass_on(d).wait_recv()
    weigh(blocks.at[2], 2, 3)

    @pl.loop(0, steps // 2)
    def _(t):
        at = pl.ds(pl.multiple_of(t * big, 16), big)
        keep(t, big, pl.ds(0, LANES), one_block(int_high[at, :], int_low[at, :], 2))

    core_start(0)
    core_add(0)
    pair_copy(0, 0).start()
    pair_copy(0, 1).start()

    def antisym(q, i, u):
        ah = q // 2
        bh = q % 2
        mirror = (c + i) % 2

        @pl.loop(0, h // 2, unroll=4)
        def _(n):
            a = u * (h // 2) + n
            plain = rows[ah, i * h + a, bh]
            turned = rows[2 + bh, pl.ds(mirror * h, h), ah, a, :]
            diff[q * 4 + i * 2 + u, pl.ds(pl.multiple_of(n * h, 8), h), :] = plain - turned

    def up_copy(q):
        return pltpu.make_async_remote_copy(
            src_ref=upward.at[q], dst_ref=below.at[q],
            send_sem=up_send.at[q], recv_sem=up_recv.at[q],
            device_id={"virt": v + 2}, device_id_type=MESH,
        )

    def down_copy(q):
        return pltpu.make_async_remote_copy(
            src_ref=downward.at[q], dst_ref=above.at[q],
            send_sem=down_send.at[q], recv_sem=down_recv.at[q],
            device_id={"virt": v - 2}, device_id_type=MESH,
        )

    def sends_up(q):
        return jnp.logical_or(z < 2, jnp.logical_and(z == 2, q // 4 % 2 == 1))

    def sends_down(q):
        return jnp.logical_or(z > 1, jnp.logical_and(z == 1, q // 8 == 0))

    def hears_below(q):
        return jnp.logical_or(inner, jnp.logical_and(z == 3, q // 4 % 2 == 1))

    def hears_above(q):
        return jnp.logical_or(inner, jnp.logical_and(z == 0, q // 8 == 0))

    def go_up(q):
        @pl.when(hears_below(q))
        def _():
            up_copy(q).wait_recv()

        @pl.when(z == 0)
        def _():
            upward[q] = diff[q]

        @pl.when(jnp.logical_and(z > 0, sends_up(q)))
        def _():
            upward[q] = diff[q] + below[q]

        @pl.when(sends_up(q))
        def _():
            up_copy(q).start()

    def go_down(q):
        @pl.when(hears_above(q))
        def _():
            down_copy(q).wait_recv()

        @pl.when(z == 3)
        def _():
            downward[q] = diff[q]

        @pl.when(jnp.logical_and(z < 3, sends_down(q)))
        def _():
            downward[q] = diff[q] + above[q]

        @pl.when(sends_down(q))
        def _():
            down_copy(q).start()

    def near(q):
        @pl.when(z < 2)
        def _():
            go_up(q)

        @pl.when(z >= 2)
        def _():
            go_down(q)

    def far(q):
        @pl.when(z < 2)
        def _():
            go_down(q)

        @pl.when(z >= 2)
        def _():
            go_up(q)

    early = [jnp.where(y == 0, t * 2 + x, x * 2 + t) for t in range(2)]
    late = [jnp.where(y == 0, t * 2 + 1 - x, (1 - x) * 2 + t) for t in range(2)]
    quads = early + late
    chunks = [q * 4 + n for q in quads for n in range(4)]
    needs = (((1, 0), (2, 0)), ((2, 1),), ((1, 1), (0, 0)), ((0, 1),))
    lag = 3
    for s in range(16):
        if s % 4 == 0:
            for n, piece in needs[s // 4]:
                pair_arrived(n, piece)
        antisym(quads[s // 4], s // 2 % 2, s % 2)
        near(chunks[s])
        if s >= lag:

            @pl.when(inner)
            def _():
                far(chunks[s - lag])

    @pl.when(jnp.logical_not(inner))
    def _():
        for s in range(16 - lag):
            far(chunks[s])

    for s in range(16 - lag, 16):
        far(chunks[s])

    def total_of(t, i):
        q = pl.ds(jnp.where(z < 2, z * 2 + t, t * 2 + z - 2) * 4 + i * 2, 2)
        low = jnp.where(z > 0, below[q], jnp.float32(0.0))
        high = jnp.where(z < 3, above[q], jnp.float32(0.0))
        return (diff[q] + low + high).reshape(h * h, LANES)

    mine = jnp.where(z < 2, c, 0)
    for t in range(2):
        other[t] = total_of(t, jnp.where(z < 2, 1 - c, 1))
    last = pltpu.make_async_remote_copy(
        src_ref=other, dst_ref=kept.at[1], send_sem=last_send, recv_sem=last_recv,
        device_id={"virt": mate}, device_id_type=MESH,
    )
    last.start()
    for t in range(2):
        kept[0, t] = total_of(t, mine)

    def put(s):
        for t in range(2):

            @pl.loop(0, h, unroll=4)
            def _(a):
                at = pl.multiple_of((a * 4 + 2 * t + s) * h, 8)
                plain = kept[s, t, pl.ds(pl.multiple_of(a * h, 8), h), :]
                turned = kept[s, t, pl.ds(a, h, stride=h), :]
                placed[pl.ds(at, h), :] = jnp.where(z < 2, plain, turned)

    put(0)
    last.wait_recv()
    put(1)

    for n in range(out_ref.shape[1] // LANES):
        at = pl.ds(n * LANES, LANES)
        out_ref[:, at] = placed[at, :].T[:count]

    last.wait_send()
    for d in range(2):
        amp_copy(d, 0).wait_send()
        amp_copy(d, 1).wait_send()
        pass_on(d).wait_send()
    for n in range(4):
        for i in range(2):
            core_copy(n, i).wait_send()
    for n in range(3):
        for piece in range(2):
            pair_copy(n, piece).wait_send()
    for q in range(16):

        @pl.when(sends_up(q))
        def _():
            up_copy(q).wait_send()

        @pl.when(sends_down(q))
        def _():
            down_copy(q).wait_send()


def ladder_of(amplitudes, integrals, tile_width):
    h = tile_width // 4
    count, depth = amplitudes.shape
    owned = integrals.shape[0]
    step = owned // 8
    f32 = jnp.float32
    bf16 = jnp.bfloat16
    dma = pltpu.SemaphoreType.DMA
    return pl.pallas_call(
        functools.partial(ladder_kernel, h),
        out_shape=jax.ShapeDtypeStruct((count, tile_width * h), f32),
        in_specs=[pl.BlockSpec(memory_space=pltpu.VMEM), pl.BlockSpec(memory_space=pl.ANY)],
        out_specs=pl.BlockSpec(memory_space=pltpu.VMEM),
        scratch_shapes=[
            pltpu.VMEM((2, step, depth), f32),
            pltpu.VMEM((owned, depth), bf16),
            pltpu.VMEM((owned, depth), bf16),
            pltpu.VMEM((3, count, depth), f32),
            pltpu.VMEM((8 * LANES, depth), bf16),
            pltpu.VMEM((2, h, 2, 2, h, 4 * LANES), f32),
            pltpu.VMEM((4, 2, h, 2, h, LANES), f32),
            pltpu.VMEM((3, 2 * h, 2, h, LANES), f32),
            pltpu.VMEM((4, 2 * h, 2, h, LANES), f32),
            pltpu.VMEM((16, h * h // 2, LANES), f32),
            pltpu.VMEM((16, h * h // 2, LANES), f32),
            pltpu.VMEM((16, h * h // 2, LANES), f32),
            pltpu.VMEM((16, h * h // 2, LANES), f32),
            pltpu.VMEM((16, h * h // 2, LANES), f32),
            pltpu.VMEM((2, 2, h * h, LANES), f32),
            pltpu.VMEM((2, h * h, LANES), f32),
            pltpu.VMEM((tile_width * h, LANES), f32),
            dma((2,)), dma((3, 2)), dma((3, 2)),
            dma((4, 2)), dma((4, 2)), dma((3, 2)), dma((3, 2)),
            dma((16,)), dma((16,)), dma((16,)), dma((16,)), dma, dma,
        ],
        compiler_params=pltpu.CompilerParams(
            collective_id=0, has_side_effects=True, vmem_limit_bytes=60 * 1024 * 1024
        ),
        name="ladder",
    )(amplitudes, integrals)


def block_body(amplitudes, integrals, eps_occ, eps_vir, pair_list):
    tile_width = eps_vir.shape[0] // 2
    first = lax.axis_index("virt") < lax.axis_size("virt") // 2
    sign = jnp.where(first, jnp.float32(1.0), jnp.float32(-1.0))
    raw = ladder_of(amplitudes, integrals, tile_width)
    raw, eps_occ, eps_vir, pair_list = lax.optimization_barrier(
        (raw, eps_occ, eps_vir, pair_list)
    )
    ladder = sign * raw
    return (ladder, updated(ladder, eps_occ, eps_vir, pair_list))


def solution(mesh):
    in_specs = (P("pair", "virt"), P("pair", "virt"), P(), P(), P("pair", None))
    out_specs = (P("pair", "virt"), P("pair", "virt"))
    fits = mesh.shape["pair"] == 4 and mesh.shape["virt"] == 8

    def body(amplitudes, integrals, eps_occ, eps_vir, pair_list):
        tiled = eps_vir.shape[0] % 64 == 0 and amplitudes.shape[0] <= LANES
        chosen = block_body if fits and tiled else any_mesh_body
        return chosen(amplitudes, integrals, eps_occ, eps_vir, pair_list)

    return jax.shard_map(body, mesh=mesh, in_specs=in_specs, out_specs=out_specs, check_vma=False)
```

profile of v0, /device:TPU:24, one launch (start us, length us, event | category | flops | bytes accessed | tf_op | source)
XLA Modules:
  0.0 77.7 jit_solution(15468828725705680275)
XLA Ops:
  0.6 0.0 copy-start
  0.6 0.0 copy-start.2
  0.7 0.0 copy-start.1
  0.7 74.6 %ladder.1 = f32[120,1024]{1,0:T(8,128)} custom-call(f32[120,1536]{1,0:T(8,128)} %amp_ref.1, f32[2048,1536]{1,0:T(8,128)} %int_ref.1), custom_call_target="tpu_custom_call" | custom-call | tf_op jit(solution)/shard_map/ladder/pallas_call | solution.py:461
  75.2 0.0 copy-done
  75.2 0.0 copy-done.1
  75.3 0.2 select_reduce_fusion
  75.4 0.0 copy-done.2
  75.4 0.1 add.22
  75.6 0.1 broadcast_add_fusion
  75.6 0.1 add.26
  75.7 2.0 %subtract_divide_fusion = (f32[120,1024]{1,0:T(8,128)}, f32[120,1024]{1,0:T(8,128)}) fusion(f32[1024]{0:T(1024)S(1)} %dynamic_slice.3, f32[120]{0:T(128)S(1)} %select_reduce_fusion, f32[120,1024]{1,0:T(8,128)} %ladder.1, f32[]{:T(128)S(6)} %select_n.11), kind=kLoop, calls=%fused_computation | loop fusion | flops 368640 | bytes 1479140 | tf_op jit(solution)/shard_map/div | solution.py:41
  (2 shorter events, 0.0 us)
Async XLA Ops:
  0.6 74.6 %copy-start = (s32[120,2]{0,1:T(2,128)S(1)}, s32[120,2]{0,1:T(2,128)}, u32[]{:S(2)}) copy-start(s32[120,2]{0,1:T(2,128)} %param.9) | copy-start | bytes 2884
  0.6 74.8 %copy-start.2 = (f32[128]{0:T(128)S(1)}, f32[128]{0:T(128)}, u32[]{:S(2)}) copy-start(f32[128]{0:T(128)} %param.8) | copy-start | bytes 1540
  0.7 74.6 %copy-start.1 = (f32[120]{0:T(128)S(1)}, f32[120]{0:T(128)}, u32[]{:S(2)}) copy-start(f32[120]{0:T(128)} %param.7) | copy-start | bytes 1444
where the time goes:
time: 78 us; the launch traced here: 77.7 us
  Pallas kernels  74.6 us (96%)
  other arithmetic  2.29 us (3%)
    pallas_call x1, Pallas kernels, ladder_of(): pl.pallas_call(functools.partial(ladder_kernel, h), out_shape=jax.ShapeDt...  74.6 us
    div x1, other arithmetic, updated(): return ladder / (pair_energy[:, None] - local_energy[None, :])  2.03 us

commit v1 on v0

--- a/solution.py
+++ b/solution.py
@@ -67,9 +67,9 @@
 
 
 def ladder_kernel(
-    h, amp_ref, int_ref, out_ref, stage, int_high, int_low, blocks, weights, ct_ref,
+    h, amp_ref, int_ref, out_ref, own, stage, int_high, int_low, blocks, weights, ct_ref,
     got, summed, rows, diff, below, above, upward, downward, kept, other, placed,
-    stage_sem, amp_send, amp_recv,
+    own_sem, stage_sem, amp_send, amp_recv,
     core_send, core_recv, pair_send, pair_recv, up_send, up_recv, down_send, down_recv,
     last_send, last_recv,
 ):
@@ -81,11 +81,15 @@
     x = r % 2
     y = r // 2
     peers = (y * 2 + (1 - x), (1 - y) * 2 + x, (1 - y) * 2 + (1 - x))
-    count, depth = amp_ref.shape
-    cut = count // 16 * 8
-    parts = (pl.ds(0, cut), pl.ds(cut, count - cut))
+    count, depth = own.shape
+    third = depth // 3
+    sizes = (third, third // 2, third, third // 2)
+    starts = (0, third, third + third // 2, 2 * third + third // 2)
     step = stage.shape[1]
     steps = int_ref.shape[0] // step
+
+    own_copy = pltpu.make_async_copy(amp_ref, own, own_sem)
+    own_copy.start()
 
     def stage_copy(t):
         return pltpu.make_async_copy(
@@ -120,36 +124,40 @@
     def _():
         pl.semaphore_wait(barrier, 5)
 
+    def columns_of(part):
+        return pl.ds(starts[part], sizes[part])
+
     def amp_copy(d, part):
         return pltpu.make_async_remote_copy(
-            src_ref=amp_ref.at[parts[part]],
-            dst_ref=blocks.at[d, parts[part]],
+            src_ref=amp_ref.at[:, columns_of(part)],
+            dst_ref=blocks.at[d, :, columns_of(part)],
             send_sem=amp_send.at[d, part],
             recv_sem=amp_recv.at[d, part],
             device_id={"pair": peers[d]},
             device_id_type=MESH,
         )
 
-    def pass_on(d):
-        return pltpu.make_async_remote_copy(
-            src_ref=blocks.at[d, parts[d]],
-            dst_ref=blocks.at[2, parts[d]],
-            send_sem=amp_send.at[2, d],
-            recv_sem=amp_recv.at[2, d],
+    def pass_on(part):
+        d = part // 2
+        return pltpu.make_async_remote_copy(
+            src_ref=blocks.at[d, :, columns_of(part)],
+            dst_ref=blocks.at[2, :, columns_of(part)],
+            send_sem=amp_send.at[2, part],
+            recv_sem=amp_recv.at[2, part],
             device_id={"pair": peers[1 - d]},
             device_id_type=MESH,
         )
 
-    for late in range(2):
+    for parts in zip((0, 1, 2, 3), (2, 0, 1, 3)):
         for d in range(2):
-            amp_copy(d, d if late == 0 else 1 - d).start()
-
-    def weigh(source, high_at, low_at):
+            amp_copy(d, parts[d]).start()
+
+    def weigh(source, high_at, low_at, start, size):
         wide = 2 * LANES
 
-        @pl.loop(0, depth // wide)
+        @pl.loop(0, size // wide)
         def _(k):
-            columns = pl.ds(pl.multiple_of(k * wide, wide), wide)
+            columns = pl.ds(pl.multiple_of(start + k * wide, wide), wide)
             value = source[:, columns]
             if count < LANES:
                 value = jnp.concatenate(
@@ -159,18 +167,21 @@
             weights[pl.ds(high_at * LANES, LANES), columns] = high
             weights[pl.ds(low_at * LANES, LANES), columns] = low
 
-    def keep(t, size, lanes, value):
+    def keep(t, size, lanes, value, first):
         per = size // (4 * h)
         i = t // (h // per)
         at = pl.multiple_of(t % (h // per) * per, per)
-        ct_ref[i, pl.ds(at, per), :, :, :, lanes] = value.reshape(per, 2, 2, h, value.shape[1])
-
-    def one_block(high, low, at):
-        both = times(high, weights[pl.ds(at * LANES, 2 * LANES), :])
-        rest = times(low, weights[pl.ds(at * LANES, LANES), :])
+        place = (i, pl.ds(at, per), slice(None), slice(None), slice(None), lanes)
+        value = value.reshape(per, 2, 2, h, value.shape[1])
+        ct_ref[place] = value if first else ct_ref[place] + value
+
+    def one_block(high, low, at, columns):
+        both = times(high, weights[pl.ds(at * LANES, 2 * LANES), columns])
+        rest = times(low, weights[pl.ds(at * LANES, LANES), columns])
         return both[:, :LANES] + both[:, LANES:] + rest
 
-    weigh(amp_ref, 0, 1)
+    own_copy.wait()
+    weigh(own, 0, 1, 0, depth)
 
     @pl.loop(0, steps)
     def _(t):
@@ -184,11 +195,8 @@
         def _():
             stage_copy(t + 2).start()
 
-        keep(t, step, pl.ds(3 * LANES, LANES), one_block(int_high[at, :], int_low[at, :], 0))
-
-    for d in range(2):
-        amp_copy(d, d).wait_recv()
-        pass_on(d).start()
+        value = one_block(int_high[at, :], int_low[at, :], 0, slice(None))
+        keep(t, step, pl.ds(3 * LANES, LANES), value, True)
 
     order = (peers[2], peers[0], peers[1], r)
 
@@ -202,80 +210,103 @@
             device_id_type=MESH,
         )
 
-    def pair_copy(n, piece):
-        bh = jnp.where(piece == 0, 1 - x, x) if n == 1 else piece
-        return pltpu.make_async_remote_copy(
-            src_ref=summed.at[n, :, bh],
-            dst_ref=rows.at[r, :, bh],
-            send_sem=pair_send.at[n, piece],
-            recv_sem=pair_recv.at[n, piece],
+    def pair_copy(n, piece, i):
+        bh = (x if n == 2 else 1 - x) if piece == 0 else (1 - x if n == 2 else x)
+        return pltpu.make_async_remote_copy(
+            src_ref=summed.at[n, pl.ds(i * h, h), bh],
+            dst_ref=rows.at[r, pl.ds(i * h, h), bh],
+            send_sem=pair_send.at[n, piece, i],
+            recv_sem=pair_recv.at[n, piece, i],
             device_id={"pair": order[n]},
             device_id_type=MESH,
         )
 
-    def pair_arrived(n, piece):
-        pair_copy(n, piece).wait_recv()
-
-    def core_start(n):
-        for i in range(2):
-            core_copy(n, i).start()
-
+    def core_add(n, i):
+        lanes = pl.ds(n * LANES, LANES)
+        core_copy(n, i).wait_recv()
+
+        @pl.loop(0, h, unroll=4)
+        def _(a):
+            for bh in range(2):
+                total = ct_ref[i, a, bh, (c + i) % 2, :, lanes] + got[n, i, a, bh]
+                if n < 3:
+                    summed[n, i * h + a, bh] = total
+                else:
+                    rows[r, i * h + a, bh] = total
+
+    big = 2 * step
     half = steps // 4
 
-    def core_add(n):
-        lanes = pl.ds(n * LANES, LANES)
-        for i in range(2):
-            core_copy(n, i).wait_recv()
-
-            @pl.loop(0, h, unroll=4)
-            def _(a):
-                for bh in range(2):
-                    total = ct_ref[i, a, bh, (c + i) % 2, :, lanes] + got[n, i, a, bh]
-                    if n < 3:
-                        summed[n, i * h + a, bh] = total
-                    else:
-                        rows[r, i * h + a, bh] = total
-
-    core_start(3)
-    for d in range(2):
-        amp_copy(d, 1 - d).wait_recv()
-        weigh(blocks.at[d], 4 + d, 6 + d)
-    big = 2 * step
-
-    for i in range(2):
+    def near_block(i, start, size, first):
+        columns = pl.ds(start, size)
 
         @pl.loop(i * half, (i + 1) * half)
         def _(t):
             at = pl.ds(pl.multiple_of(t * big, 16), big)
-            near_high = weights[pl.ds(4 * LANES, 2 * LANES), :]
-            near_low = weights[pl.ds(6 * LANES, 2 * LANES), :]
-            value = times(int_high[at, :], near_high) + times(int_high[at, :], near_low)
-            value = value + times(int_low[at, :], near_high)
-            keep(t, big, pl.ds(LANES, 2 * LANES), value)
-
+            near_high = weights[pl.ds(4 * LANES, 2 * LANES), columns]
+            near_low = weights[pl.ds(6 * LANES, 2 * LANES), columns]
+            value = times(int_high[at, columns], near_high)
+            value = value + times(int_high[at, columns], near_low)
+            value = value + times(int_low[at, columns], near_high)
+            keep(t, big, pl.ds(LANES, 2 * LANES), value, first)
+
+    for i in range(2):
+        core_copy(3, i).start()
+    amp_copy(0, 0).wait_recv()
+    pass_on(0).start()
+    amp_copy(1, 2).wait_recv()
+    pass_on(2).start()
+    amp_copy(1, 0).wait_recv()
+    for d in range(2):
+        weigh(blocks.at[d], 4 + d, 6 + d, starts[0], sizes[0])
+    for i in range(2):
+        near_block(i, starts[0], sizes[0], True)
+    amp_copy(0, 1).wait_recv()
+    pass_on(1).start()
+    for i in range(2):
+        core_add(3, i)
+    amp_copy(1, 1).wait_recv()
+    amp_copy(0, 2).wait_recv()
+    for d in range(2):
+        weigh(blocks.at[d], 4 + d, 6 + d, starts[1], sizes[1] + sizes[2])
+    for i in range(2):
+        near_block(i, starts[1], sizes[1] + sizes[2], False)
+    amp_copy(1, 3).wait_recv()
+    pass_on(3).start()
+    amp_copy(0, 3).wait_recv()
+    for d in range(2):
+        weigh(blocks.at[d], 4 + d, 6 + d, starts[3], sizes[3])
+    for i in range(2):
+        near_block(i, starts[3], sizes[3], False)
+        core_copy(2, i).start()
         core_copy(1, i).start()
-        core_copy(2, i).start()
-
-    core_add(1)
-    pair_copy(1, 0).start()
-    core_add(2)
-    pair_copy(2, 0).start()
-    pair_copy(2, 1).start()
-    pair_copy(1, 1).start()
-    core_add(3)
-    for d in range(2):
-        pass_on(d).wait_recv()
-    weigh(blocks.at[2], 2, 3)
-
-    @pl.loop(0, steps // 2)
-    def _(t):
-        at = pl.ds(pl.multiple_of(t * big, 16), big)
-        keep(t, big, pl.ds(0, LANES), one_block(int_high[at, :], int_low[at, :], 2))
-
-    core_start(0)
-    core_add(0)
-    pair_copy(0, 0).start()
-    pair_copy(0, 1).start()
+    for i in range(2):
+        core_add(2, i)
+        pair_copy(2, 0, i).start()
+        core_add(1, i)
+        pair_copy(1, 0, i).start()
+    for n in (2, 1):
+        for i in range(2):
+            pair_copy(n, 1, i).start()
+
+    def far_block(i, parts, first):
+        @pl.loop(i * half, (i + 1) * half)
+        def _(t):
+            at = pl.ds(pl.multiple_of(t * big, 16), big)
+            values = [
+                one_block(int_high[at, columns_of(p)], int_low[at, columns_of(p)], 2, columns_of(p))
+                for p in parts
+            ]
+            keep(t, big, pl.ds(0, LANES), values[0] + values[1], first)
+
+    for parts in ((0, 2), (1, 3)):
+        for p in parts:
+            pass_on(p).wait_recv()
+            weigh(blocks.at[2], 2, 3, starts[p], sizes[p])
+        for i in range(2):
+            far_block(i, parts, parts[0] == 0)
+            if parts[0] == 1:
+                core_copy(0, i).start()
 
     def antisym(q, i, u):
         ah = q // 2
@@ -367,18 +398,32 @@
         def _():
             go_up(q)
 
-    early = [jnp.where(y == 0, t * 2 + x, x * 2 + t) for t in range(2)]
-    late = [jnp.where(y == 0, t * 2 + 1 - x, (1 - x) * 2 + t) for t in range(2)]
-    quads = early + late
-    chunks = [q * 4 + n for q in quads for n in range(4)]
-    needs = (((1, 0), (2, 0)), ((2, 1),), ((1, 1), (0, 0)), ((0, 1),))
+    alike = x * 3
+    unlike = (1 - x) * 3
+    mixed_near = jnp.where(y == 0, unlike // 3 * 2 + x, x * 2 + 1 - x)
+    mixed_far = jnp.where(y == 0, x * 2 + 1 - x, (1 - x) * 2 + x)
+    quads = (alike, mixed_near, mixed_far, unlike)
+    turns = [jnp.where(y == 0, (t + c) % 2, t) for t in range(2)]
+    chunks = [q * 4 + turns[t] * 2 + u for q in quads for t in range(2) for u in range(2)]
+    needs = (
+        ((2, 0, 0),), ((2, 0, 1),),
+        ((1, 0, 0), (1, 0, 1), (2, 1, 0)), ((2, 1, 1),),
+        ((0, 0, 0),), ((0, 0, 1),),
+        ((1, 1, 0), (1, 1, 1), (0, 1, 0)), ((0, 1, 1),),
+    )
     lag = 3
     for s in range(16):
-        if s % 4 == 0:
-            for n, piece in needs[s // 4]:
-                pair_arrived(n, piece)
-        antisym(quads[s // 4], s // 2 % 2, s % 2)
+        if s % 2 == 0:
+            for n, piece, i in needs[s // 2]:
+                pair_copy(n, piece, i).wait_recv()
+        antisym(quads[s // 4], turns[s // 2 % 2], s % 2)
         near(chunks[s])
+        if s == 1:
+            for i in range(2):
+                core_add(0, i)
+            for piece in range(2):
+                for i in range(2):
+                    pair_copy(0, piece, i).start()
         if s >= lag:
 
             @pl.when(inner)
@@ -400,45 +445,51 @@
         return (diff[q] + low + high).reshape(h * h, LANES)
 
     mine = jnp.where(z < 2, c, 0)
+
+    def last_copy(t):
+        return pltpu.make_async_remote_copy(
+            src_ref=other.at[t], dst_ref=kept.at[1, t],
+            send_sem=last_send.at[t], recv_sem=last_recv.at[t],
+            device_id={"virt": mate}, device_id_type=MESH,
+        )
+
     for t in range(2):
         other[t] = total_of(t, jnp.where(z < 2, 1 - c, 1))
-    last = pltpu.make_async_remote_copy(
-        src_ref=other, dst_ref=kept.at[1], send_sem=last_send, recv_sem=last_recv,
-        device_id={"virt": mate}, device_id_type=MESH,
-    )
-    last.start()
+        last_copy(t).start()
     for t in range(2):
         kept[0, t] = total_of(t, mine)
 
-    def put(s):
-        for t in range(2):
-
-            @pl.loop(0, h, unroll=4)
-            def _(a):
-                at = pl.multiple_of((a * 4 + 2 * t + s) * h, 8)
-                plain = kept[s, t, pl.ds(pl.multiple_of(a * h, 8), h), :]
-                turned = kept[s, t, pl.ds(a, h, stride=h), :]
-                placed[pl.ds(at, h), :] = jnp.where(z < 2, plain, turned)
-
-    put(0)
-    last.wait_recv()
-    put(1)
+    def put(s, t):
+        @pl.loop(0, h, unroll=4)
+        def _(a):
+            at = pl.multiple_of((a * 4 + 2 * t + s) * h, 8)
+            plain = kept[s, t, pl.ds(pl.multiple_of(a * h, 8), h), :]
+            turned = kept[s, t, pl.ds(a, h, stride=h), :]
+            placed[pl.ds(at, h), :] = jnp.where(z < 2, plain, turned)
+
+    for t in range(2):
+        put(0, t)
+    for t in range(2):
+        last_copy(t).wait_recv()
+        put(1, t)
 
     for n in range(out_ref.shape[1] // LANES):
         at = pl.ds(n * LANES, LANES)
         out_ref[:, at] = placed[at, :].T[:count]
 
-    last.wait_send()
-    for d in range(2):
-        amp_copy(d, 0).wait_send()
-        amp_copy(d, 1).wait_send()
-        pass_on(d).wait_send()
+    for t in range(2):
+        last_copy(t).wait_send()
+    for part in range(4):
+        for d in range(2):
+            amp_copy(d, part).wait_send()
+        pass_on(part).wait_send()
     for n in range(4):
         for i in range(2):
             core_copy(n, i).wait_send()
     for n in range(3):
         for piece in range(2):
-            pair_copy(n, piece).wait_send()
+            for i in range(2):
+                pair_copy(n, piece, i).wait_send()
     for q in range(16):
 
         @pl.when(sends_up(q))
@@ -460,10 +511,11 @@
     dma = pltpu.SemaphoreType.DMA
     return pl.pallas_call(
         functools.partial(ladder_kernel, h),
-        out_shape=jax.ShapeDtypeStruct((count, tile_width * h), f32),
-        in_specs=[pl.BlockSpec(memory_space=pltpu.VMEM), pl.BlockSpec(memory_space=pl.ANY)],
+        out_shape=pltpu.VMEM((count, tile_width * h), f32),
+        in_specs=[pl.BlockSpec(memory_space=pl.ANY), pl.BlockSpec(memory_space=pl.ANY)],
         out_specs=pl.BlockSpec(memory_space=pltpu.VMEM),
         scratch_shapes=[
+            pltpu.VMEM((count, depth), f32),
             pltpu.VMEM((2, step, depth), f32),
             pltpu.VMEM((owned, depth), bf16),
             pltpu.VMEM((owned, depth), bf16),
@@ -481,12 +533,12 @@
             pltpu.VMEM((2, 2, h * h, LANES), f32),
             pltpu.VMEM((2, h * h, LANES), f32),
             pltpu.VMEM((tile_width * h, LANES), f32),
-            dma((2,)), dma((3, 2)), dma((3, 2)),
-            dma((4, 2)), dma((4, 2)), dma((3, 2)), dma((3, 2)),
-            dma((16,)), dma((16,)), dma((16,)), dma((16,)), dma, dma,
+            dma, dma((2,)), dma((3, 4)), dma((3, 4)),
+            dma((4, 2)), dma((4, 2)), dma((3, 2, 2)), dma((3, 2, 2)),
+            dma((16,)), dma((16,)), dma((16,)), dma((16,)), dma((2,)), dma((2,)),
         ],
         compiler_params=pltpu.CompilerParams(
-            collective_id=0, has_side_effects=True, vmem_limit_bytes=60 * 1024 * 1024
+            collective_id=0, has_side_effects=True, vmem_limit_bytes=58 * 1024 * 1024
         ),
         name="ladder",
     )(amplitudes, integrals)
@@ -511,6 +563,7 @@
 
     def body(amplitudes, integrals, eps_occ, eps_vir, pair_list):
         tiled = eps_vir.shape[0] % 64 == 0 and amplitudes.shape[0] <= LANES
+        tiled = tiled and amplitudes.shape[1] % (12 * LANES) == 0
         chosen = block_body if fits and tiled else any_mesh_body
         return chosen(amplitudes, integrals, eps_occ, eps_vir, pair_list)
 

time: 78 us -> 69.1 us (0.89)
  the two profiles are of different devices: /device:TPU:24 before, /device:TPU:7 now
where the time goes in v1:
time: 69.1 us; the launch traced here: 68.7 us
  Pallas kernels  66.5 us (96%)
  other arithmetic  1.26 us (2%)
  between operations  0.7 us (1%)
    pallas_call x1, Pallas kernels, ladder_of(): pl.pallas_call(functools.partial(ladder_kernel, h), out_shape=pltpu.VMEM(...  66.5 us

profile of v1, /device:TPU:7, one launch (start us, length us, event | category | flops | bytes accessed | tf_op | source)
XLA Modules:
  0.0 68.7 jit_solution(17182424496020214521)
XLA Ops:
  0.6 0.0 copy-start
  0.6 0.0 copy-start.2
  0.7 0.0 copy-start.1
  0.7 66.5 %ladder.1 = f32[120,1024]{1,0:T(8,128)S(1)} custom-call(f32[120,1536]{1,0:T(8,128)} %amp_ref.1, f32[2048,1536]{1,0:T(8,128)} %int_ref.1), custom_call_target="tpu_custom_call" | custom-call | tf_op jit(solution)/shard_map/ladder/pallas_call | solution.py:512
  67.2 0.0 copy-done
  67.2 0.0 copy-done.1
  67.2 0.2 select_reduce_fusion
  67.4 0.0 copy-done.2
  67.4 0.1 add.22
  67.5 0.1 broadcast_add_fusion
  67.6 0.1 add.26
  67.7 1.0 %subtract_divide_fusion = (f32[120,1024]{1,0:T(8,128)}, f32[120,1024]{1,0:T(8,128)}) fusion(f32[1024]{0:T(1024)S(1)} %dynamic_slice.3, f32[120]{0:T(128)S(1)} %select_reduce_fusion, f32[120,1024]{1,0:T(8,128)S(1)} %ladder.1, f32[]{:T(128)S(6)} %select_n.11), kind=kLoop, calls=%fused_computation | loop fusion | flops 368640 | bytes 1479140 | tf_op jit(solution)/shard_map/div | solution.py:41
  (2 shorter events, 0.0 us)
Async XLA Ops:
  0.6 66.6 %copy-start = (s32[120,2]{0,1:T(2,128)S(1)}, s32[120,2]{0,1:T(2,128)}, u32[]{:S(2)}) copy-start(s32[120,2]{0,1:T(2,128)} %param.9) | copy-start | bytes 2884
  0.6 66.7 %copy-start.2 = (f32[128]{0:T(128)S(1)}, f32[128]{0:T(128)}, u32[]{:S(2)}) copy-start(f32[128]{0:T(128)} %param.8) | copy-start | bytes 1540
  0.7 66.5 %copy-start.1 = (f32[120]{0:T(128)S(1)}, f32[120]{0:T(128)}, u32[]{:S(2)}) copy-start(f32[120]{0:T(128)} %param.7) | copy-start | bytes 1444

commit v2 on v1

--- a/solution.py
+++ b/solution.py
@@ -68,10 +68,10 @@
 
 def ladder_kernel(
     h, amp_ref, int_ref, out_ref, own, stage, int_high, int_low, blocks, weights, ct_ref,
-    got, summed, rows, diff, below, above, upward, downward, kept, other, placed,
+    got, summed, rows, diff, below, above, sums, kept, other, placed,
     own_sem, stage_sem, amp_send, amp_recv,
-    core_send, core_recv, pair_send, pair_recv, up_send, up_recv, down_send, down_recv,
-    last_send, last_recv,
+    core_send, core_recv, pair_send, pair_recv,
+    main_send, side_send, below_recv, above_recv, last_send, last_recv,
 ):
     r = lax.axis_index("pair")
     v = lax.axis_index("virt")
@@ -114,15 +114,17 @@
     def _():
         pl.semaphore_signal(barrier, inc=1, device_id={"virt": v - 2}, device_id_type=MESH)
 
+    across = (v + 4) % 8
+    pl.semaphore_signal(barrier, inc=1, device_id={"virt": across}, device_id_type=MESH)
     inner = jnp.logical_and(z > 0, z < 3)
 
     @pl.when(inner)
     def _():
-        pl.semaphore_wait(barrier, 6)
+        pl.semaphore_wait(barrier, 7)
 
     @pl.when(jnp.logical_not(inner))
     def _():
-        pl.semaphore_wait(barrier, 5)
+        pl.semaphore_wait(barrier, 6)
 
     def columns_of(part):
         return pl.ds(starts[part], sizes[part])
@@ -308,116 +310,158 @@
             if parts[0] == 1:
                 core_copy(0, i).start()
 
-    def antisym(q, i, u):
+    def antisym(q, i, u, size):
         ah = q // 2
         bh = q % 2
         mirror = (c + i) % 2
-
-        @pl.loop(0, h // 2, unroll=4)
+        rises = h // 4
+
+        @pl.loop(0, size * rises, unroll=4)
         def _(n):
-            a = u * (h // 2) + n
+            a = u * rises + n
             plain = rows[ah, i * h + a, bh]
             turned = rows[2 + bh, pl.ds(mirror * h, h), ah, a, :]
-            diff[q * 4 + i * 2 + u, pl.ds(pl.multiple_of(n * h, 8), h), :] = plain - turned
-
-    def up_copy(q):
+            at = q * 8 + i * 4 + u + n // rises
+            diff[at, pl.ds(pl.multiple_of(n % rises * h, 8), h), :] = plain - turned
+
+    def main_copy(upwards, q, k, size):
+        far_up = jnp.where(z == 0, 0, q % 2)
+        far_down = jnp.where(z == 3, 0, 1 - q // 2)
+        at = pl.ds(k, size)
         return pltpu.make_async_remote_copy(
-            src_ref=upward.at[q], dst_ref=below.at[q],
-            send_sem=up_send.at[q], recv_sem=up_recv.at[q],
-            device_id={"virt": v + 2}, device_id_type=MESH,
-        )
-
-    def down_copy(q):
+            src_ref=sums.at[at],
+            dst_ref=(below if upwards else above).at[at],
+            send_sem=main_send.at[k],
+            recv_sem=(below_recv if upwards else above_recv).at[k],
+            device_id={"virt": v + 2 + 2 * far_up if upwards else v - 2 - 2 * far_down},
+            device_id_type=MESH,
+        )
+
+    def side_copy(upwards, k, size):
+        at = pl.ds(k, size)
         return pltpu.make_async_remote_copy(
-            src_ref=downward.at[q], dst_ref=above.at[q],
-            send_sem=down_send.at[q], recv_sem=down_recv.at[q],
-            device_id={"virt": v - 2}, device_id_type=MESH,
-        )
-
-    def sends_up(q):
-        return jnp.logical_or(z < 2, jnp.logical_and(z == 2, q // 4 % 2 == 1))
-
-    def sends_down(q):
-        return jnp.logical_or(z > 1, jnp.logical_and(z == 1, q // 8 == 0))
-
-    def hears_below(q):
-        return jnp.logical_or(inner, jnp.logical_and(z == 3, q // 4 % 2 == 1))
-
-    def hears_above(q):
-        return jnp.logical_or(inner, jnp.logical_and(z == 0, q // 8 == 0))
-
-    def go_up(q):
-        @pl.when(hears_below(q))
-        def _():
-            up_copy(q).wait_recv()
-
-        @pl.when(z == 0)
-        def _():
-            upward[q] = diff[q]
-
-        @pl.when(jnp.logical_and(z > 0, sends_up(q)))
-        def _():
-            upward[q] = diff[q] + below[q]
-
-        @pl.when(sends_up(q))
-        def _():
-            up_copy(q).start()
-
-    def go_down(q):
-        @pl.when(hears_above(q))
-        def _():
-            down_copy(q).wait_recv()
-
-        @pl.when(z == 3)
-        def _():
-            downward[q] = diff[q]
-
-        @pl.when(jnp.logical_and(z < 3, sends_down(q)))
-        def _():
-            downward[q] = diff[q] + above[q]
-
-        @pl.when(sends_down(q))
-        def _():
-            down_copy(q).start()
-
-    def near(q):
+            src_ref=diff.at[at],
+            dst_ref=(above if upwards else below).at[at],
+            send_sem=side_send.at[k],
+            recv_sem=(above_recv if upwards else below_recv).at[k],
+            device_id={"virt": v + 2 if upwards else v - 2},
+            device_id_type=MESH,
+        )
+
+    def side_down(q):
+        return jnp.logical_and(z == 1, q // 2 == 0)
+
+    def side_up(q):
+        return jnp.logical_and(z == 2, q % 2 == 1)
+
+    def near(q, k, size):
+        at = pl.ds(k, size)
+
+        @pl.when(side_down(q))
+        def _():
+            side_copy(False, k, size).start()
+
+        @pl.when(side_up(q))
+        def _():
+            side_copy(True, k, size).start()
+
+        @pl.when(jnp.logical_not(inner))
+        def _():
+            sums[at] = diff[at]
+
+        @pl.when(z == 1)
+        def _():
+            main_copy(True, q, k, size).wait_recv()
+            sums[at] = diff[at] + below[at]
+
+        @pl.when(z == 2)
+        def _():
+            main_copy(False, q, k, size).wait_recv()
+            sums[at] = diff[at] + above[at]
+
         @pl.when(z < 2)
         def _():
-            go_up(q)
+            main_copy(True, q, k, size).start()
 
         @pl.when(z >= 2)
         def _():
-            go_down(q)
-
-    def far(q):
-        @pl.when(z < 2)
-        def _():
-            go_down(q)
-
-        @pl.when(z >= 2)
-        def _():
-            go_up(q)
+            main_copy(False, q, k, size).start()
+
+    def last_copy(t, u, size):
+        at = pl.ds(pl.multiple_of(u * piece_rows, 8), size * piece_rows)
+        return pltpu.make_async_remote_copy(
+            src_ref=other.at[t, at],
+            dst_ref=kept.at[1, t, at],
+            send_sem=last_send.at[t, u],
+            recv_sem=last_recv.at[t, u],
+            device_id={"virt": mate},
+            device_id_type=MESH,
+        )
+
+    piece_rows = h * h // 4
+    ours = jnp.where(z < 2, c, 0)
+
+    def owned_here(q):
+        return jnp.where(z < 2, q // 2 == z, q % 2 == z - 2)
+
+    def place_of(q):
+        return jnp.where(z < 2, q % 2, q // 2)
+
+    def finish(q, i, u, size):
+        k = q * 8 + i * 4 + u
+        at = pl.ds(k, size)
+        t = place_of(q)
+        to = pl.ds(pl.multiple_of(u * piece_rows, 8), size * piece_rows)
+
+        @pl.when(owned_here(q))
+        def _():
+            @pl.when(z != 1)
+            def _():
+                main_copy(True, q, k, size).wait_recv()
+
+            @pl.when(z != 2)
+            def _():
+                main_copy(False, q, k, size).wait_recv()
+
+            total = (diff[at] + below[at] + above[at]).reshape(size * piece_rows, LANES)
+
+            @pl.when(i == ours)
+            def _():
+                kept[0, t, to] = total
+
+            @pl.when(i != ours)
+            def _():
+                other[t, to] = total
+                last_copy(t, u, size).start()
 
     alike = x * 3
     unlike = (1 - x) * 3
-    mixed_near = jnp.where(y == 0, unlike // 3 * 2 + x, x * 2 + 1 - x)
+    mixed_near = jnp.where(y == 0, (1 - x) * 2 + x, x * 2 + 1 - x)
     mixed_far = jnp.where(y == 0, x * 2 + 1 - x, (1 - x) * 2 + x)
     quads = (alike, mixed_near, mixed_far, unlike)
     turns = [jnp.where(y == 0, (t + c) % 2, t) for t in range(2)]
-    chunks = [q * 4 + turns[t] * 2 + u for q in quads for t in range(2) for u in range(2)]
+    mate_turns = [jnp.where(y == 0, (t + 1 - c) % 2, t) for t in range(2)]
+    mate_ours = jnp.where(z < 2, 1 - c, 0)
     needs = (
         ((2, 0, 0),), ((2, 0, 1),),
         ((1, 0, 0), (1, 0, 1), (2, 1, 0)), ((2, 1, 1),),
         ((0, 0, 0),), ((0, 0, 1),),
         ((1, 1, 0), (1, 1, 1), (0, 1, 0)), ((0, 1, 1),),
     )
-    lag = 3
-    for s in range(16):
-        if s % 2 == 0:
-            for n, piece, i in needs[s // 2]:
+    todo = []
+    for g in range(4):
+        for t in range(2):
+            size = 1 if g == 3 else 2
+            for u in range(0, 4, size):
+                todo.append((g, t, u, size))
+    lag = 6
+    for s, (g, t, u, size) in enumerate(todo):
+        q = quads[g]
+        if u == 0:
+            for n, piece, i in needs[g * 2 + t]:
                 pair_copy(n, piece, i).wait_recv()
-        antisym(quads[s // 4], turns[s // 2 % 2], s % 2)
-        near(chunks[s])
+        antisym(q, turns[t], u, size)
+        near(q, q * 8 + turns[t] * 4 + u, size)
         if s == 1:
             for i in range(2):
                 core_add(0, i)
@@ -425,39 +469,19 @@
                 for i in range(2):
                     pair_copy(0, piece, i).start()
         if s >= lag:
+            eg, et, eu, esize = todo[s - lag]
 
             @pl.when(inner)
             def _():
-                far(chunks[s - lag])
+                finish(quads[eg], turns[et], eu, esize)
 
     @pl.when(jnp.logical_not(inner))
     def _():
-        for s in range(16 - lag):
-            far(chunks[s])
-
-    for s in range(16 - lag, 16):
-        far(chunks[s])
-
-    def total_of(t, i):
-        q = pl.ds(jnp.where(z < 2, z * 2 + t, t * 2 + z - 2) * 4 + i * 2, 2)
-        low = jnp.where(z > 0, below[q], jnp.float32(0.0))
-        high = jnp.where(z < 3, above[q], jnp.float32(0.0))
-        return (diff[q] + low + high).reshape(h * h, LANES)
-
-    mine = jnp.where(z < 2, c, 0)
-
-    def last_copy(t):
-        return pltpu.make_async_remote_copy(
-            src_ref=other.at[t], dst_ref=kept.at[1, t],
-            send_sem=last_send.at[t], recv_sem=last_recv.at[t],
-            device_id={"virt": mate}, device_id_type=MESH,
-        )
-
-    for t in range(2):
-        other[t] = total_of(t, jnp.where(z < 2, 1 - c, 1))
-        last_copy(t).start()
-    for t in range(2):
-        kept[0, t] = total_of(t, mine)
+        for g, t, u, size in todo[: len(todo) - lag]:
+            finish(quads[g], turns[t], u, size)
+
+    for g, t, u, size in todo[len(todo) - lag :]:
+        finish(quads[g], turns[t], u, size)
 
     def put(s, t):
         @pl.loop(0, h, unroll=4)
@@ -469,16 +493,20 @@
 
     for t in range(2):
         put(0, t)
+    for g, t, u, size in todo:
+        q = quads[g]
+
+        @pl.when(jnp.logical_and(owned_here(q), mate_turns[t] != mate_ours))
+        def _():
+            last_copy(place_of(q), u, size).wait_recv()
+
     for t in range(2):
-        last_copy(t).wait_recv()
         put(1, t)
 
     for n in range(out_ref.shape[1] // LANES):
         at = pl.ds(n * LANES, LANES)
         out_ref[:, at] = placed[at, :].T[:count]
 
-    for t in range(2):
-        last_copy(t).wait_send()
     for part in range(4):
         for d in range(2):
             amp_copy(d, part).wait_send()
@@ -490,15 +518,18 @@
         for piece in range(2):
             for i in range(2):
                 pair_copy(n, piece, i).wait_send()
-    for q in range(16):
-
-        @pl.when(sends_up(q))
-        def _():
-            up_copy(q).wait_send()
-
-        @pl.when(sends_down(q))
-        def _():
-            down_copy(q).wait_send()
+    for g, t, u, size in todo:
+        q = quads[g]
+        k = q * 8 + turns[t] * 4 + u
+        main_copy(True, q, k, size).wait_send()
+
+        @pl.when(jnp.logical_or(side_down(q), side_up(q)))
+        def _():
+            side_copy(True, k, size).wait_send()
+
+        @pl.when(jnp.logical_and(owned_here(q), turns[t] != ours))
+        def _():
+            last_copy(place_of(q), u, size).wait_send()
 
 
 def ladder_of(amplitudes, integrals, tile_width):
@@ -525,17 +556,16 @@
             pltpu.VMEM((4, 2, h, 2, h, LANES), f32),
             pltpu.VMEM((3, 2 * h, 2, h, LANES), f32),
             pltpu.VMEM((4, 2 * h, 2, h, LANES), f32),
-            pltpu.VMEM((16, h * h // 2, LANES), f32),
-            pltpu.VMEM((16, h * h // 2, LANES), f32),
-            pltpu.VMEM((16, h * h // 2, LANES), f32),
-            pltpu.VMEM((16, h * h // 2, LANES), f32),
-            pltpu.VMEM((16, h * h // 2, LANES), f32),
+            pltpu.VMEM((32, h * h // 4, LANES), f32),
+            pltpu.VMEM((32, h * h // 4, LANES), f32),
+            pltpu.VMEM((32, h * h // 4, LANES), f32),
+            pltpu.VMEM((32, h * h // 4, LANES), f32),
             pltpu.VMEM((2, 2, h * h, LANES), f32),
             pltpu.VMEM((2, h * h, LANES), f32),
             pltpu.VMEM((tile_width * h, LANES), f32),
             dma, dma((2,)), dma((3, 4)), dma((3, 4)),
             dma((4, 2)), dma((4, 2)), dma((3, 2, 2)), dma((3, 2, 2)),
-            dma((16,)), dma((16,)), dma((16,)), dma((16,)), dma((2,)), dma((2,)),
+            dma((32,)), dma((32,)), dma((32,)), dma((32,)), dma((2, 4)), dma((2, 4)),
         ],
         compiler_params=pltpu.CompilerParams(
             collective_id=0, has_side_effects=True, vmem_limit_bytes=58 * 1024 * 1024

time: 69.1 us -> 74.8 us (1.082)
  Pallas kernels: 66.5 us -> 72.4 us
    pallas_call x1, Pallas kernels: 66.5 us -> 72.4 us  [ladder_of(): pl.pallas_call(functools.partial(ladder_kernel, h), out_shape=pltpu.VMEM(...]
where the time goes in v2:
time: 74.8 us; the launch traced here: 74.6 us
  Pallas kernels  72.4 us (97%)
  other arithmetic  1.26 us (2%)
    pallas_call x1, Pallas kernels, ladder_of(): pl.pallas_call(functools.partial(ladder_kernel, h), out_shape=pltpu.VMEM(...  72.4 us

profile of v2, /device:TPU:7, one launch (start us, length us, event | category | flops | bytes accessed | tf_op | source)
XLA Modules:
  0.0 74.6 jit_solution(7161055948432018800)
XLA Ops:
  0.6 0.0 copy-start
  0.6 0.0 copy-start.2
  0.7 0.0 copy-start.1
  0.7 72.4 %ladder.1 = f32[120,1024]{1,0:T(8,128)S(1)} custom-call(f32[120,1536]{1,0:T(8,128)} %amp_ref.1, f32[2048,1536]{1,0:T(8,128)} %int_ref.1), custom_call_target="tpu_custom_call" | custom-call | tf_op jit(solution)/shard_map/ladder/pallas_call | solution.py:543
  73.1 0.0 copy-done
  73.1 0.0 copy-done.1
  73.1 0.2 select_reduce_fusion
  73.3 0.0 copy-done.2
  73.3 0.1 add.22
  73.4 0.1 broadcast_add_fusion
  73.5 0.1 add.26
  73.6 1.0 %subtract_divide_fusion = (f32[120,1024]{1,0:T(8,128)}, f32[120,1024]{1,0:T(8,128)}) fusion(f32[1024]{0:T(1024)S(1)} %dynamic_slice.3, f32[120]{0:T(128)S(1)} %select_reduce_fusion, f32[120,1024]{1,0:T(8,128)S(1)} %ladder.1, f32[]{:T(128)S(6)} %select_n.11), kind=kLoop, calls=%fused_computation | loop fusion | flops 368640 | bytes 1479140 | tf_op jit(solution)/shard_map/div | solution.py:41
  (2 shorter events, 0.0 us)
Async XLA Ops:
  0.6 72.5 %copy-start = (s32[120,2]{0,1:T(2,128)S(1)}, s32[120,2]{0,1:T(2,128)}, u32[]{:S(2)}) copy-start(s32[120,2]{0,1:T(2,128)} %param.9) | copy-start | bytes 2884
  0.6 72.7 %copy-start.2 = (f32[128]{0:T(128)S(1)}, f32[128]{0:T(128)}, u32[]{:S(2)}) copy-start(f32[128]{0:T(128)} %param.8) | copy-start | bytes 1540
  0.7 72.5 %copy-start.1 = (f32[120]{0:T(128)S(1)}, f32[120]{0:T(128)}, u32[]{:S(2)}) copy-start(f32[120]{0:T(128)} %param.7) | copy-start | bytes 1444

commit v3 on v2

--- a/solution.py
+++ b/solution.py
@@ -68,7 +68,7 @@
 
 def ladder_kernel(
     h, amp_ref, int_ref, out_ref, own, stage, int_high, int_low, blocks, weights, ct_ref,
-    got, summed, rows, diff, below, above, sums, kept, other, placed,
+    got, summed, rows, diff, below, above, sums, relayed, kept, other, placed,
     own_sem, stage_sem, amp_send, amp_recv,
     core_send, core_recv, pair_send, pair_recv,
     main_send, side_send, below_recv, above_recv, last_send, last_recv,
@@ -133,7 +133,7 @@
         return pltpu.make_async_remote_copy(
             src_ref=amp_ref.at[:, columns_of(part)],
             dst_ref=blocks.at[d, :, columns_of(part)],
-            send_sem=amp_send.at[d, part],
+            send_sem=amp_send,
             recv_sem=amp_recv.at[d, part],
             device_id={"pair": peers[d]},
             device_id_type=MESH,
@@ -144,7 +144,7 @@
         return pltpu.make_async_remote_copy(
             src_ref=blocks.at[d, :, columns_of(part)],
             dst_ref=blocks.at[2, :, columns_of(part)],
-            send_sem=amp_send.at[2, part],
+            send_sem=amp_send,
             recv_sem=amp_recv.at[2, part],
             device_id={"pair": peers[1 - d]},
             device_id_type=MESH,
@@ -206,7 +206,7 @@
         return pltpu.make_async_remote_copy(
             src_ref=ct_ref.at[i, :, :, (1 - c + i) % 2, :, pl.ds(n * LANES, LANES)],
             dst_ref=got.at[n, i],
-            send_sem=core_send.at[n, i],
+            send_sem=core_send,
             recv_sem=core_recv.at[n, i],
             device_id={"virt": mate},
             device_id_type=MESH,
@@ -217,7 +217,7 @@
         return pltpu.make_async_remote_copy(
             src_ref=summed.at[n, pl.ds(i * h, h), bh],
             dst_ref=rows.at[r, pl.ds(i * h, h), bh],
-            send_sem=pair_send.at[n, piece, i],
+            send_sem=pair_send,
             recv_sem=pair_recv.at[n, piece, i],
             device_id={"pair": order[n]},
             device_id_type=MESH,
@@ -324,26 +324,37 @@
             at = q * 8 + i * 4 + u + n // rises
             diff[at, pl.ds(pl.multiple_of(n % rises * h, 8), h), :] = plain - turned
 
-    def main_copy(upwards, q, k, size):
-        far_up = jnp.where(z == 0, 0, q % 2)
-        far_down = jnp.where(z == 3, 0, 1 - q // 2)
+    def main_copy(upwards, q, k, size, direct, step_at):
+        far_up = jnp.where(z == 0, 0, q % 2) if direct else 0
+        far_down = jnp.where(z == 3, 0, 1 - q // 2) if direct else 0
         at = pl.ds(k, size)
         return pltpu.make_async_remote_copy(
             src_ref=sums.at[at],
             dst_ref=(below if upwards else above).at[at],
-            send_sem=main_send.at[k],
-            recv_sem=(below_recv if upwards else above_recv).at[k],
+            send_sem=main_send,
+            recv_sem=(below_recv if upwards else above_recv).at[step_at],
             device_id={"virt": v + 2 + 2 * far_up if upwards else v - 2 - 2 * far_down},
             device_id_type=MESH,
         )
 
-    def side_copy(upwards, k, size):
+    def relay_copy(upwards, k, size, step_at):
+        at = pl.ds(k, size)
+        return pltpu.make_async_remote_copy(
+            src_ref=relayed.at[at],
+            dst_ref=(below if upwards else above).at[at],
+            send_sem=side_send,
+            recv_sem=(below_recv if upwards else above_recv).at[step_at],
+            device_id={"virt": v + 2 if upwards else v - 2},
+            device_id_type=MESH,
+        )
+
+    def side_copy(upwards, k, size, step_at):
         at = pl.ds(k, size)
         return pltpu.make_async_remote_copy(
             src_ref=diff.at[at],
             dst_ref=(above if upwards else below).at[at],
-            send_sem=side_send.at[k],
-            recv_sem=(above_recv if upwards else below_recv).at[k],
+            send_sem=side_send,
+            recv_sem=(above_recv if upwards else below_recv).at[step_at],
             device_id={"virt": v + 2 if upwards else v - 2},
             device_id_type=MESH,
         )
@@ -354,45 +365,67 @@
     def side_up(q):
         return jnp.logical_and(z == 2, q % 2 == 1)
 
-    def near(q, k, size):
+    def near(q, k, size, direct, step_at):
         at = pl.ds(k, size)
+        if direct:
+
+            @pl.when(side_down(q))
+            def _():
+                side_copy(False, k, size, step_at).start()
+
+            @pl.when(side_up(q))
+            def _():
+                side_copy(True, k, size, step_at).start()
+
+        @pl.when(jnp.logical_not(inner))
+        def _():
+            sums[at] = diff[at]
+
+        @pl.when(z == 1)
+        def _():
+            main_copy(True, q, k, size, direct, step_at).wait_recv()
+            sums[at] = diff[at] + below[at]
+
+        @pl.when(z == 2)
+        def _():
+            main_copy(False, q, k, size, direct, step_at).wait_recv()
+            sums[at] = diff[at] + above[at]
+
+        @pl.when(z < 2)
+        def _():
+            main_copy(True, q, k, size, direct, step_at).start()
+
+        @pl.when(z >= 2)
+        def _():
+            main_copy(False, q, k, size, direct, step_at).start()
+
+    def relay(q, k, size, step_at):
+        at = pl.ds(k, size)
+
+        @pl.when(z == 1)
+        def _():
+            relay_copy(False, k, size, step_at).wait_recv()
+
+        @pl.when(z == 2)
+        def _():
+            relay_copy(True, k, size, step_at).wait_recv()
 
         @pl.when(side_down(q))
         def _():
-            side_copy(False, k, size).start()
+            relayed[at] = diff[at] + above[at]
+            relay_copy(False, k, size, step_at).start()
 
         @pl.when(side_up(q))
         def _():
-            side_copy(True, k, size).start()
-
-        @pl.when(jnp.logical_not(inner))
-        def _():
-            sums[at] = diff[at]
-
-        @pl.when(z == 1)
-        def _():
-            main_copy(True, q, k, size).wait_recv()
-            sums[at] = diff[at] + below[at]
-
-        @pl.when(z == 2)
-        def _():
-            main_copy(False, q, k, size).wait_recv()
-            sums[at] = diff[at] + above[at]
-
-        @pl.when(z < 2)
-        def _():
-            main_copy(True, q, k, size).start()
-
-        @pl.when(z >= 2)
-        def _():
-            main_copy(False, q, k, size).start()
+            relayed[at] = diff[at] + below[at]
+            relay_copy(True, k, size, step_at).start()
 
     def last_copy(t, u, size):
         at = pl.ds(pl.multiple_of(u * piece_rows, 8), size * piece_rows)
         return pltpu.make_async_remote_copy(
             src_ref=other.at[t, at],
             dst_ref=kept.at[1, t, at],
-            send_sem=last_send.at[t, u],
+            send_sem=last_send,
             recv_sem=last_recv.at[t, u],
             device_id={"virt": mate},
             device_id_type=MESH,
@@ -407,7 +440,7 @@
     def place_of(q):
         return jnp.where(z < 2, q % 2, q // 2)
 
-    def finish(q, i, u, size):
+    def finish(q, i, u, size, direct, step_at):
         k = q * 8 + i * 4 + u
         at = pl.ds(k, size)
         t = place_of(q)
@@ -415,15 +448,20 @@
 
         @pl.when(owned_here(q))
         def _():
-            @pl.when(z != 1)
+            @pl.when(z != 1 if direct else z == 3)
             def _():
-                main_copy(True, q, k, size).wait_recv()
-
-            @pl.when(z != 2)
+                main_copy(True, q, k, size, direct, step_at).wait_recv()
+
+            @pl.when(z != 2 if direct else z == 0)
             def _():
-                main_copy(False, q, k, size).wait_recv()
-
-            total = (diff[at] + below[at] + above[at]).reshape(size * piece_rows, LANES)
+                main_copy(False, q, k, size, direct, step_at).wait_recv()
+
+            low = below[at]
+            high = above[at]
+            if not direct:
+                low = jnp.where(z > 0, low, jnp.float32(0.0))
+                high = jnp.where(z < 3, high, jnp.float32(0.0))
+            total = (diff[at] + low + high).reshape(size * piece_rows, LANES)
 
             @pl.when(i == ours)
             def _():
@@ -451,17 +489,19 @@
     todo = []
     for g in range(4):
         for t in range(2):
-            size = 1 if g == 3 else 2
+            direct = g == 3 and t == 1
+            size = 1 if direct else 2
             for u in range(0, 4, size):
-                todo.append((g, t, u, size))
-    lag = 6
-    for s, (g, t, u, size) in enumerate(todo):
+                todo.append((g, t, u, size, direct))
+    lag = 4
+    later = 6
+    for s, (g, t, u, size, direct) in enumerate(todo):
         q = quads[g]
         if u == 0:
             for n, piece, i in needs[g * 2 + t]:
                 pair_copy(n, piece, i).wait_recv()
         antisym(q, turns[t], u, size)
-        near(q, q * 8 + turns[t] * 4 + u, size)
+        near(q, q * 8 + turns[t] * 4 + u, size, direct, s)
         if s == 1:
             for i in range(2):
                 core_add(0, i)
@@ -469,19 +509,28 @@
                 for i in range(2):
                     pair_copy(0, piece, i).start()
         if s >= lag:
-            eg, et, eu, esize = todo[s - lag]
+            eg, et, eu, esize, edirect = todo[s - lag]
+            if not edirect:
+
+                @pl.when(inner)
+                def _():
+                    relay(quads[eg], quads[eg] * 8 + turns[et] * 4 + eu, esize, s - lag)
+
+        if s >= later:
+            eg, et, eu, esize, edirect = todo[s - later]
 
             @pl.when(inner)
             def _():
-                finish(quads[eg], turns[et], eu, esize)
+                finish(quads[eg], turns[et], eu, esize, edirect, s - later)
 
     @pl.when(jnp.logical_not(inner))
     def _():
-        for g, t, u, size in todo[: len(todo) - lag]:
-            finish(quads[g], turns[t], u, size)
-
-    for g, t, u, size in todo[len(todo) - lag :]:
-        finish(quads[g], turns[t], u, size)
+        for s, (g, t, u, size, direct) in enumerate(todo[: len(todo) - later]):
+            finish(quads[g], turns[t], u, size, direct, s)
+
+    for s in range(len(todo) - later, len(todo)):
+        g, t, u, size, direct = todo[s]
+        finish(quads[g], turns[t], u, size, direct, s)
 
     def put(s, t):
         @pl.loop(0, h, unroll=4)
@@ -493,7 +542,7 @@
 
     for t in range(2):
         put(0, t)
-    for g, t, u, size in todo:
+    for g, t, u, size, direct in todo:
         q = quads[g]
 
         @pl.when(jnp.logical_and(owned_here(q), mate_turns[t] != mate_ours))
@@ -507,29 +556,21 @@
         at = pl.ds(n * LANES, LANES)
         out_ref[:, at] = placed[at, :].T[:count]
 
-    for part in range(4):
-        for d in range(2):
-            amp_copy(d, part).wait_send()
-        pass_on(part).wait_send()
-    for n in range(4):
-        for i in range(2):
-            core_copy(n, i).wait_send()
-    for n in range(3):
-        for piece in range(2):
-            for i in range(2):
-                pair_copy(n, piece, i).wait_send()
-    for g, t, u, size in todo:
-        q = quads[g]
-        k = q * 8 + turns[t] * 4 + u
-        main_copy(True, q, k, size).wait_send()
-
-        @pl.when(jnp.logical_or(side_down(q), side_up(q)))
-        def _():
-            side_copy(True, k, size).wait_send()
-
-        @pl.when(jnp.logical_and(owned_here(q), turns[t] != ours))
-        def _():
-            last_copy(place_of(q), u, size).wait_send()
+    def wait_sent(buffer, sem):
+        pltpu.make_async_remote_copy(
+            src_ref=buffer, dst_ref=buffer, send_sem=sem, recv_sem=own_sem,
+            device_id={"virt": mate}, device_id_type=MESH,
+        ).wait_send()
+
+    wait_sent(blocks, amp_send)
+    wait_sent(got, core_send)
+    wait_sent(summed, pair_send)
+    wait_sent(sums, main_send)
+    wait_sent(other, last_send)
+
+    @pl.when(inner)
+    def _():
+        wait_sent(relayed.at[pl.ds(0, 16)], side_send)
 
 
 def ladder_of(amplitudes, integrals, tile_width):
@@ -560,12 +601,13 @@
             pltpu.VMEM((32, h * h // 4, LANES), f32),
             pltpu.VMEM((32, h * h // 4, LANES), f32),
             pltpu.VMEM((32, h * h // 4, LANES), f32),
+            pltpu.VMEM((32, h * h // 4, LANES), f32),
             pltpu.VMEM((2, 2, h * h, LANES), f32),
             pltpu.VMEM((2, h * h, LANES), f32),
             pltpu.VMEM((tile_width * h, LANES), f32),
-            dma, dma((2,)), dma((3, 4)), dma((3, 4)),
-            dma((4, 2)), dma((4, 2)), dma((3, 2, 2)), dma((3, 2, 2)),
-            dma((32,)), dma((32,)), dma((32,)), dma((32,)), dma((2, 4)), dma((2, 4)),
+            dma, dma((2,)), dma, dma((3, 4)),
+            dma, dma((4, 2)), dma, dma((3, 2, 2)),
+            dma, dma, dma((18,)), dma((18,)), dma, dma((2, 4)),
         ],
         compiler_params=pltpu.CompilerParams(
             collective_id=0, has_side_effects=True, vmem_limit_bytes=58 * 1024 * 1024

time: 74.8 us -> 71.5 us (0.956)
  Pallas kernels: 72.4 us -> 69.1 us
    pallas_call x1, Pallas kernels: 72.4 us -> 69.1 us  [ladder_of(): pl.pallas_call(functools.partial(ladder_kernel, h), out_shape=pltpu.VMEM(...]
where the time goes in v3:
time: 71.5 us; the launch traced here: 71.3 us
  Pallas kernels  69.1 us (97%)
  other arithmetic  1.26 us (2%)
    pallas_call x1, Pallas kernels, ladder_of(): pl.pallas_call(functools.partial(ladder_kernel, h), out_shape=pltpu.VMEM(...  69.1 us

profile of v3, /device:TPU:7, one launch (start us, length us, event | category | flops | bytes accessed | tf_op | source)
XLA Modules:
  0.0 71.3 jit_solution(7955072461783529189)
XLA Ops:
  0.6 0.0 copy-start
  0.6 0.0 copy-start.2
  0.7 0.0 copy-start.1
  0.7 69.1 %ladder.1 = f32[120,1024]{1,0:T(8,128)S(1)} custom-call(f32[120,1536]{1,0:T(8,128)} %amp_ref.1, f32[2048,1536]{1,0:T(8,128)} %int_ref.1), custom_call_target="tpu_custom_call" | custom-call | tf_op jit(solution)/shard_map/ladder/pallas_call | solution.py:584
  69.8 0.0 copy-done
  69.8 0.0 copy-done.1
  69.8 0.2 select_reduce_fusion
  70.0 0.0 copy-done.2
  70.0 0.1 add.22
  70.1 0.1 broadcast_add_fusion
  70.2 0.1 add.26
  70.3 1.0 %subtract_divide_fusion = (f32[120,1024]{1,0:T(8,128)}, f32[120,1024]{1,0:T(8,128)}) fusion(f32[1024]{0:T(1024)S(1)} %dynamic_slice.3, f32[120]{0:T(128)S(1)} %select_reduce_fusion, f32[120,1024]{1,0:T(8,128)S(1)} %ladder.1, f32[]{:T(128)S(6)} %select_n.11), kind=kLoop, calls=%fused_computation | loop fusion | flops 368640 | bytes 1479140 | tf_op jit(solution)/shard_map/div | solution.py:41
  (2 shorter events, 0.0 us)
Async XLA Ops:
  0.6 69.2 %copy-start = (s32[120,2]{0,1:T(2,128)S(1)}, s32[120,2]{0,1:T(2,128)}, u32[]{:S(2)}) copy-start(s32[120,2]{0,1:T(2,128)} %param.9) | copy-start | bytes 2884
  0.6 69.4 %copy-start.2 = (f32[128]{0:T(128)S(1)}, f32[128]{0:T(128)}, u32[]{:S(2)}) copy-start(f32[128]{0:T(128)} %param.8) | copy-start | bytes 1540
  0.7 69.2 %copy-start.1 = (f32[120]{0:T(128)S(1)}, f32[120]{0:T(128)}, u32[]{:S(2)}) copy-start(f32[120]{0:T(128)} %param.7) | copy-start | bytes 1444

commit v4 on v3

--- a/solution.py
+++ b/solution.py
@@ -114,17 +114,15 @@
     def _():
         pl.semaphore_signal(barrier, inc=1, device_id={"virt": v - 2}, device_id_type=MESH)
 
-    across = (v + 4) % 8
-    pl.semaphore_signal(barrier, inc=1, device_id={"virt": across}, device_id_type=MESH)
     inner = jnp.logical_and(z > 0, z < 3)
 
     @pl.when(inner)
     def _():
-        pl.semaphore_wait(barrier, 7)
+        pl.semaphore_wait(barrier, 6)
 
     @pl.when(jnp.logical_not(inner))
     def _():
-        pl.semaphore_wait(barrier, 6)
+        pl.semaphore_wait(barrier, 5)
 
     def columns_of(part):
         return pl.ds(starts[part], sizes[part])
@@ -324,16 +322,14 @@
             at = q * 8 + i * 4 + u + n // rises
             diff[at, pl.ds(pl.multiple_of(n % rises * h, 8), h), :] = plain - turned
 
-    def main_copy(upwards, q, k, size, direct, step_at):
-        far_up = jnp.where(z == 0, 0, q % 2) if direct else 0
-        far_down = jnp.where(z == 3, 0, 1 - q // 2) if direct else 0
+    def main_copy(upwards, q, k, size, step_at):
         at = pl.ds(k, size)
         return pltpu.make_async_remote_copy(
             src_ref=sums.at[at],
             dst_ref=(below if upwards else above).at[at],
             send_sem=main_send,
             recv_sem=(below_recv if upwards else above_recv).at[step_at],
-            device_id={"virt": v + 2 + 2 * far_up if upwards else v - 2 - 2 * far_down},
+            device_id={"virt": v + 2 if upwards else v - 2},
             device_id_type=MESH,
         )
 
@@ -348,56 +344,35 @@
             device_id_type=MESH,
         )
 
-    def side_copy(upwards, k, size, step_at):
+    def sends_down(q):
+        return jnp.logical_and(z == 1, q // 2 == 0)
+
+    def sends_up(q):
+        return jnp.logical_and(z == 2, q % 2 == 1)
+
+    def near(q, k, size, step_at):
         at = pl.ds(k, size)
-        return pltpu.make_async_remote_copy(
-            src_ref=diff.at[at],
-            dst_ref=(above if upwards else below).at[at],
-            send_sem=side_send,
-            recv_sem=(above_recv if upwards else below_recv).at[step_at],
-            device_id={"virt": v + 2 if upwards else v - 2},
-            device_id_type=MESH,
-        )
-
-    def side_down(q):
-        return jnp.logical_and(z == 1, q // 2 == 0)
-
-    def side_up(q):
-        return jnp.logical_and(z == 2, q % 2 == 1)
-
-    def near(q, k, size, direct, step_at):
-        at = pl.ds(k, size)
-        if direct:
-
-            @pl.when(side_down(q))
-            def _():
-                side_copy(False, k, size, step_at).start()
-
-            @pl.when(side_up(q))
-            def _():
-                side_copy(True, k, size, step_at).start()
-
         @pl.when(jnp.logical_not(inner))
         def _():
             sums[at] = diff[at]
 
         @pl.when(z == 1)
         def _():
-            main_copy(True, q, k, size, direct, step_at).wait_recv()
+            main_copy(True, q, k, size, step_at).wait_recv()
             sums[at] = diff[at] + below[at]
 
         @pl.when(z == 2)
         def _():
-            main_copy(False, q, k, size, direct, step_at).wait_recv()
+            main_copy(False, q, k, size, step_at).wait_recv()
             sums[at] = diff[at] + above[at]
 
         @pl.when(z < 2)
         def _():
-            main_copy(True, q, k, size, direct, step_at).start()
+            main_copy(True, q, k, size, step_at).start()
 
         @pl.when(z >= 2)
         def _():
-            main_copy(False, q, k, size, direct, step_at).start()
+            main_copy(False, q, k, size, step_at).start()
 
     def relay(q, k, size, step_at):
         at = pl.ds(k, size)
@@ -410,12 +385,12 @@
         def _():
             relay_copy(True, k, size, step_at).wait_recv()
 
-        @pl.when(side_down(q))
+        @pl.when(sends_down(q))
         def _():
             relayed[at] = diff[at] + above[at]
             relay_copy(False, k, size, step_at).start()
 
-        @pl.when(side_up(q))
+        @pl.when(sends_up(q))
         def _():
             relayed[at] = diff[at] + below[at]
             relay_copy(True, k, size, step_at).start()
@@ -440,7 +415,7 @@
     def place_of(q):
         return jnp.where(z < 2, q % 2, q // 2)
 
-    def finish(q, i, u, size, direct, step_at):
+    def finish(q, i, u, size, step_at):
         k = q * 8 + i * 4 + u
         at = pl.ds(k, size)
         t = place_of(q)
@@ -448,19 +423,16 @@
 
         @pl.when(owned_here(q))
         def _():
-            @pl.when(z != 1 if direct else z == 3)
+            @pl.when(z == 3)
             def _():
-                main_copy(True, q, k, size, direct, step_at).wait_recv()
-
-            @pl.when(z != 2 if direct else z == 0)
+                main_copy(True, q, k, size, step_at).wait_recv()
+
+            @pl.when(z == 0)
             def _():
-                main_copy(False, q, k, size, direct, step_at).wait_recv()
-
-            low = below[at]
-            high = above[at]
-            if not direct:
-                low = jnp.where(z > 0, low, jnp.float32(0.0))
-                high = jnp.where(z < 3, high, jnp.float32(0.0))
+                main_copy(False, q, k, size, step_at).wait_recv()
+
+            low = jnp.where(z > 0, below[at], jnp.float32(0.0))
+            high = jnp.where(z < 3, above[at], jnp.float32(0.0))
             total = (diff[at] + low + high).reshape(size * piece_rows, LANES)
 
             @pl.when(i == ours)
@@ -489,19 +461,18 @@
     todo = []
     for g in range(4):
         for t in range(2):
-            direct = g == 3 and t == 1
-            size = 1 if direct else 2
+            size = 1 if g == 3 and t == 1 else 2
             for u in range(0, 4, size):
-                todo.append((g, t, u, size, direct))
-    lag = 4
+                todo.append((g, t, u, size))
+    lag = 3
     later = 6
-    for s, (g, t, u, size, direct) in enumerate(todo):
+    for s, (g, t, u, size) in enumerate(todo):
         q = quads[g]
         if u == 0:
             for n, piece, i in needs[g * 2 + t]:
                 pair_copy(n, piece, i).wait_recv()
         antisym(q, turns[t], u, size)
-        near(q, q * 8 + turns[t] * 4 + u, size, direct, s)
+        near(q, q * 8 + turns[t] * 4 + u, size, s)
         if s == 1:
             for i in range(2):
                 core_add(0, i)
@@ -509,28 +480,33 @@
                 for i in range(2):
                     pair_copy(0, piece, i).start()
         if s >= lag:
-            eg, et, eu, esize, edirect = todo[s - lag]
-            if not edirect:
-
-                @pl.when(inner)
-                def _():
-                    relay(quads[eg], quads[eg] * 8 + turns[et] * 4 + eu, esize, s - lag)
-
-        if s >= later:
-            eg, et, eu, esize, edirect = todo[s - later]
+            eg, et, eu, esize = todo[s - lag]
 
             @pl.when(inner)
             def _():
-                finish(quads[eg], turns[et], eu, esize, edirect, s - later)
+                relay(quads[eg], quads[eg] * 8 + turns[et] * 4 + eu, esize, s - lag)
+
+        if s >= later:
+            eg, et, eu, esize = todo[s - later]
+
+            @pl.when(inner)
+            def _():
+                finish(quads[eg], turns[et], eu, esize, s - later)
 
     @pl.when(jnp.logical_not(inner))
     def _():
-        for s, (g, t, u, size, direct) in enumerate(todo[: len(todo) - later]):
-            finish(quads[g], turns[t], u, size, direct, s)
+        for s, (g, t, u, size) in enumerate(todo[: len(todo) - later]):
+            finish(quads[g], turns[t], u, size, s)
 
     for s in range(len(todo) - later, len(todo)):
-        g, t, u, size, direct = todo[s]
-        finish(quads[g], turns[t], u, size, direct, s)
+        g, t, u, size = todo[s]
+        if s >= len(todo) - lag:
+
+            @pl.when(inner)
+            def _():
+                relay(quads[g], quads[g] * 8 + turns[t] * 4 + u, size, s)
+
+        finish(quads[g], turns[t], u, size, s)
 
     def put(s, t):
         @pl.loop(0, h, unroll=4)
@@ -542,7 +518,7 @@
 
     for t in range(2):
         put(0, t)
-    for g, t, u, size, direct in todo:
+    for g, t, u, size in todo:
         q = quads[g]
 
         @pl.when(jnp.logical_and(owned_here(q), mate_turns[t] != mate_ours))

time: 71.5 us -> 68 us (0.951)
  Pallas kernels: 69.1 us -> 65.7 us
    pallas_call x1, Pallas kernels: 69.1 us -> 65.7 us  [ladder_of(): pl.pallas_call(functools.partial(ladder_kernel, h), out_shape=pltpu.VMEM(...]
where the time goes in v4:
time: 68 us; the launch traced here: 67.9 us
  Pallas kernels  65.7 us (97%)
  other arithmetic  1.26 us (2%)
  between operations  0.7 us (1%)
    pallas_call x1, Pallas kernels, ladder_of(): pl.pallas_call(functools.partial(ladder_kernel, h), out_shape=pltpu.VMEM(...  65.7 us

profile of v4, /device:TPU:7, one launch (start us, length us, event | category | flops | bytes accessed | tf_op | source)
XLA Modules:
  0.0 67.9 jit_solution(2466545633758260807)
XLA Ops:
  0.6 0.0 copy-start
  0.6 0.0 copy-start.2
  0.7 0.0 copy-start.1
  0.7 65.7 %ladder.1 = f32[120,1024]{1,0:T(8,128)S(1)} custom-call(f32[120,1536]{1,0:T(8,128)} %amp_ref.1, f32[2048,1536]{1,0:T(8,128)} %int_ref.1), custom_call_target="tpu_custom_call" | custom-call | tf_op jit(solution)/shard_map/ladder/pallas_call | solution.py:560
  66.4 0.0 copy-done
  66.4 0.0 copy-done.1
  66.4 0.2 select_reduce_fusion
  66.6 0.0 copy-done.2
  66.6 0.1 add.22
  66.7 0.1 broadcast_add_fusion
  66.8 0.1 add.26
  66.9 1.0 %subtract_divide_fusion = (f32[120,1024]{1,0:T(8,128)}, f32[120,1024]{1,0:T(8,128)}) fusion(f32[1024]{0:T(1024)S(1)} %dynamic_slice.3, f32[120]{0:T(128)S(1)} %select_reduce_fusion, f32[120,1024]{1,0:T(8,128)S(1)} %ladder.1, f32[]{:T(128)S(6)} %select_n.11), kind=kLoop, calls=%fused_computation | loop fusion | flops 368640 | bytes 1479140 | tf_op jit(solution)/shard_map/div | solution.py:41
  (2 shorter events, 0.0 us)
Async XLA Ops:
  0.6 65.7 %copy-start = (s32[120,2]{0,1:T(2,128)S(1)}, s32[120,2]{0,1:T(2,128)}, u32[]{:S(2)}) copy-start(s32[120,2]{0,1:T(2,128)} %param.9) | copy-start | bytes 2884
  0.6 65.9 %copy-start.2 = (f32[128]{0:T(128)S(1)}, f32[128]{0:T(128)}, u32[]{:S(2)}) copy-start(f32[128]{0:T(128)} %param.8) | copy-start | bytes 1540
  0.7 65.7 %copy-start.1 = (f32[120]{0:T(128)S(1)}, f32[120]{0:T(128)}, u32[]{:S(2)}) copy-start(f32[120]{0:T(128)} %param.7) | copy-start | bytes 1444

commit v5 on v4

--- a/solution.py
+++ b/solution.py
@@ -461,7 +461,7 @@
     todo = []
     for g in range(4):
         for t in range(2):
-            size = 1 if g == 3 and t == 1 else 2
+            size = 2
             for u in range(0, 4, size):
                 todo.append((g, t, u, size))
     lag = 3
@@ -583,7 +583,7 @@
             pltpu.VMEM((tile_width * h, LANES), f32),
             dma, dma((2,)), dma, dma((3, 4)),
             dma, dma((4, 2)), dma, dma((3, 2, 2)),
-            dma, dma, dma((18,)), dma((18,)), dma, dma((2, 4)),
+            dma, dma, dma((16,)), dma((16,)), dma, dma((2, 4)),
         ],
         compiler_params=pltpu.CompilerParams(
             collective_id=0, has_side_effects=True, vmem_limit_bytes=58 * 1024 * 1024

time: 68 us -> 68.3 us (level)
  no operation moved by 1% of the time
where the time goes in v5:
time: 68.3 us; the launch traced here: 67.9 us
  Pallas kernels  65.7 us (96%)
  other arithmetic  1.26 us (2%)
  between operations  0.7 us (1%)
    pallas_call x1, Pallas kernels, ladder_of(): pl.pallas_call(functools.partial(ladder_kernel, h), out_shape=pltpu.VMEM(...  65.7 us

profile of v5, /device:TPU:7, one launch (start us, length us, event | category | flops | bytes accessed | tf_op | source)
XLA Modules:
  0.0 67.9 jit_solution(1859282666602070259)
XLA Ops:
  0.6 0.0 copy-start
  0.6 0.0 copy-start.2
  0.7 0.0 copy-start.1
  0.7 65.7 %ladder.1 = f32[120,1024]{1,0:T(8,128)S(1)} custom-call(f32[120,1536]{1,0:T(8,128)} %amp_ref.1, f32[2048,1536]{1,0:T(8,128)} %int_ref.1), custom_call_target="tpu_custom_call" | custom-call | tf_op jit(solution)/shard_map/ladder/pallas_call | solution.py:560
  66.4 0.0 copy-done
  66.4 0.0 copy-done.1
  66.4 0.2 select_reduce_fusion
  66.6 0.0 copy-done.2
  66.6 0.1 add.22
  66.7 0.1 broadcast_add_fusion
  66.8 0.1 add.26
  66.9 1.0 %subtract_divide_fusion = (f32[120,1024]{1,0:T(8,128)}, f32[120,1024]{1,0:T(8,128)}) fusion(f32[1024]{0:T(1024)S(1)} %dynamic_slice.3, f32[120]{0:T(128)S(1)} %select_reduce_fusion, f32[120,1024]{1,0:T(8,128)S(1)} %ladder.1, f32[]{:T(128)S(6)} %select_n.11), kind=kLoop, calls=%fused_computation | loop fusion | flops 368640 | bytes 1479140 | tf_op jit(solution)/shard_map/div | solution.py:41
  (2 shorter events, 0.0 us)
Async XLA Ops:
  0.6 65.8 %copy-start = (s32[120,2]{0,1:T(2,128)S(1)}, s32[120,2]{0,1:T(2,128)}, u32[]{:S(2)}) copy-start(s32[120,2]{0,1:T(2,128)} %param.9) | copy-start | bytes 2884
  0.6 66.0 %copy-start.2 = (f32[128]{0:T(128)S(1)}, f32[128]{0:T(128)}, u32[]{:S(2)}) copy-start(f32[128]{0:T(128)} %param.8) | copy-start | bytes 1540
  0.7 65.8 %copy-start.1 = (f32[120]{0:T(128)S(1)}, f32[120]{0:T(128)}, u32[]{:S(2)}) copy-start(f32[120]{0:T(128)} %param.7) | copy-start | bytes 1444

commit v6 on v4

--- a/solution.py
+++ b/solution.py
@@ -322,10 +322,10 @@
             at = q * 8 + i * 4 + u + n // rises
             diff[at, pl.ds(pl.multiple_of(n % rises * h, 8), h), :] = plain - turned
 
-    def main_copy(upwards, q, k, size, step_at):
+    def main_copy(upwards, q, k, size, step_at, source=None):
         at = pl.ds(k, size)
         return pltpu.make_async_remote_copy(
-            src_ref=sums.at[at],
+            src_ref=(sums if source is None else source).at[at],
             dst_ref=(below if upwards else above).at[at],
             send_sem=main_send,
             recv_sem=(below_recv if upwards else above_recv).at[step_at],
@@ -352,27 +352,25 @@
 
     def near(q, k, size, step_at):
         at = pl.ds(k, size)
-        @pl.when(jnp.logical_not(inner))
-        def _():
-            sums[at] = diff[at]
+        @pl.when(z == 0)
+        def _():
+            main_copy(True, q, k, size, step_at, diff).start()
 
         @pl.when(z == 1)
         def _():
             main_copy(True, q, k, size, step_at).wait_recv()
             sums[at] = diff[at] + below[at]
+            main_copy(True, q, k, size, step_at).start()
 
         @pl.when(z == 2)
         def _():
             main_copy(False, q, k, size, step_at).wait_recv()
             sums[at] = diff[at] + above[at]
-
-        @pl.when(z < 2)
-        def _():
-            main_copy(True, q, k, size, step_at).start()
-
-        @pl.when(z >= 2)
-        def _():
             main_copy(False, q, k, size, step_at).start()
+
+        @pl.when(z == 3)
+        def _():
+            main_copy(False, q, k, size, step_at, diff).start()
 
     def relay(q, k, size, step_at):
         at = pl.ds(k, size)
@@ -401,7 +399,7 @@
             src_ref=other.at[t, at],
             dst_ref=kept.at[1, t, at],
             send_sem=last_send,
-            recv_sem=last_recv.at[t, u],
+            recv_sem=last_recv,
             device_id={"virt": mate},
             device_id_type=MESH,
         )
@@ -450,8 +448,6 @@
     mixed_far = jnp.where(y == 0, x * 2 + 1 - x, (1 - x) * 2 + x)
     quads = (alike, mixed_near, mixed_far, unlike)
     turns = [jnp.where(y == 0, (t + c) % 2, t) for t in range(2)]
-    mate_turns = [jnp.where(y == 0, (t + 1 - c) % 2, t) for t in range(2)]
-    mate_ours = jnp.where(z < 2, 1 - c, 0)
     needs = (
         ((2, 0, 0),), ((2, 0, 1),),
         ((1, 0, 0), (1, 0, 1), (2, 1, 0)), ((2, 1, 1),),
@@ -518,13 +514,10 @@
 
     for t in range(2):
         put(0, t)
-    for g, t, u, size in todo:
-        q = quads[g]
-
-        @pl.when(jnp.logical_and(owned_here(q), mate_turns[t] != mate_ours))
-        def _():
-            last_copy(place_of(q), u, size).wait_recv()
-
+    pltpu.make_async_remote_copy(
+        src_ref=other, dst_ref=kept.at[1], send_sem=last_send, recv_sem=last_recv,
+        device_id={"virt": mate}, device_id_type=MESH,
+    ).wait_recv()
     for t in range(2):
         put(1, t)
 
@@ -583,7 +576,7 @@
             pltpu.VMEM((tile_width * h, LANES), f32),
             dma, dma((2,)), dma, dma((3, 4)),
             dma, dma((4, 2)), dma, dma((3, 2, 2)),
-            dma, dma, dma((18,)), dma((18,)), dma, dma((2, 4)),
+            dma, dma, dma((18,)), dma((18,)), dma, dma,
         ],
         compiler_params=pltpu.CompilerParams(
             collective_id=0, has_side_effects=True, vmem_limit_bytes=58 * 1024 * 1024

time: 68 us -> 68 us (level)
  no operation moved by 1% of the time
where the time goes in v6:
time: 68 us; the launch traced here: 67.8 us
  Pallas kernels  65.6 us (96%)
  other arithmetic  1.26 us (2%)
  between operations  0.7 us (1%)
    pallas_call x1, Pallas kernels, ladder_of(): pl.pallas_call(functools.partial(ladder_kernel, h), out_shape=pltpu.VMEM(...  65.6 us

profile of v6, /device:TPU:7, one launch (start us, length us, event | category | flops | bytes accessed | tf_op | source)
XLA Modules:
  0.0 67.8 jit_solution(15552485592418333078)
XLA Ops:
  0.6 0.0 copy-start
  0.6 0.0 copy-start.2
  0.7 0.0 copy-start.1
  0.7 65.6 %ladder.1 = f32[120,1024]{1,0:T(8,128)S(1)} custom-call(f32[120,1536]{1,0:T(8,128)} %amp_ref.1, f32[2048,1536]{1,0:T(8,128)} %int_ref.1), custom_call_target="tpu_custom_call" | custom-call | tf_op jit(solution)/shard_map/ladder/pallas_call | solution.py:553
  66.3 0.0 copy-done
  66.3 0.0 copy-done.1
  66.3 0.2 select_reduce_fusion
  66.5 0.0 copy-done.2
  66.5 0.1 add.22
  66.6 0.1 broadcast_add_fusion
  66.7 0.1 add.26
  66.8 1.0 %subtract_divide_fusion = (f32[120,1024]{1,0:T(8,128)}, f32[120,1024]{1,0:T(8,128)}) fusion(f32[1024]{0:T(1024)S(1)} %dynamic_slice.3, f32[120]{0:T(128)S(1)} %select_reduce_fusion, f32[120,1024]{1,0:T(8,128)S(1)} %ladder.1, f32[]{:T(128)S(6)} %select_n.11), kind=kLoop, calls=%fused_computation | loop fusion | flops 368640 | bytes 1479140 | tf_op jit(solution)/shard_map/div | solution.py:41
  (2 shorter events, 0.0 us)
Async XLA Ops:
  0.6 65.7 %copy-start = (s32[120,2]{0,1:T(2,128)S(1)}, s32[120,2]{0,1:T(2,128)}, u32[]{:S(2)}) copy-start(s32[120,2]{0,1:T(2,128)} %param.9) | copy-start | bytes 2884
  0.6 65.9 %copy-start.2 = (f32[128]{0:T(128)S(1)}, f32[128]{0:T(128)}, u32[]{:S(2)}) copy-start(f32[128]{0:T(128)} %param.8) | copy-start | bytes 1540
  0.7 65.7 %copy-start.1 = (f32[120]{0:T(128)S(1)}, f32[120]{0:T(128)}, u32[]{:S(2)}) copy-start(f32[120]{0:T(128)} %param.7) | copy-start | bytes 1444
